TPU v7x, 32 devices: a whole 2x2x4 slice. The times are simulated.
32 devices in a mesh: groups: 2 (over x), orb: 16 (over z, y, core).
Axes of the slice: x: 2, y: 2, z: 4, core: 2. Of those that a mesh axis runs over, the one named last changes fastest.
Arguments:
- walkers: bfloat16 [256, 512, 64], P('groups', 'orb'), parts along dimension 0, may hold values from -6 to 6
- cholesky: bfloat16 [2048, 512, 512], P('groups', 'orb'), parts along dimension 0, may hold values from -0.013671875 to 0.013671875
- rotated: bfloat16 [2048, 512, 64], P('groups', 'orb'), parts along dimension 0, may hold values from -0.0068359375 to 0.0068359375
- field_noise: bfloat16 [512, 1024], P('groups'), parts along dimension 0, may hold values from -6 to 6
- sources: int32 [512], P('groups'), parts along dimension 0, may hold values from -1 to 127, as said below
Outputs:
- new_walkers: bfloat16 [512, 512, 64], P('groups', 'orb'), parts along dimension 0
- log_weight: float32 [512], P('groups'), parts along dimension 0
There are 2 independent parts, one for each index of `groups`. A program takes and returns all parts, laid end to end along the dimension named above; each array names one. Nothing has to cross between parts.
Inputs may be any that keep to these rules, and one draw needn't show every extreme that they name: sources[s] names the old walker copied into slot s, or -1 for an empty slot; slot s belongs to owner s // 16, and an owner's live slots come first; exactly 128 slots are live in all; in every draw some owner has all 16 slots live.
All inputs are finite; a program needn't handle non-finite values.
Results may differ from a plain program's by a relative error of at most 0.0085.
Values may be sent and summed in bfloat16 or wider, within the bound.
No kernel may reach another device: no remote copies, remote signals or barrier semaphores. Data moves between devices by JAX's collectives and lax.ppermute only.
A program may use at most 128 MiB of HBM per device.

v0:
```python
import functools

import jax
import jax.numpy as jnp
from jax import lax
from jax.experimental import pallas as pl
from jax.experimental.pallas import tpu as pltpu
from jax.sharding import PartitionSpec as P


TERMS = 6
ROWS = 8
LANES = 256
F32 = jnp.float32
BF16 = jnp.bfloat16


def hop(value, mask):
    size = lax.axis_size("orb")
    return lax.ppermute(value, "orb", [(i, i ^ mask) for i in range(size)])


def block_potential(fields, chol):
    swapped = jnp.swapaxes(chol, 0, 1)
    parts = [
        jnp.dot(fields, swapped[i], preferred_element_type=F32) for i in range(ROWS)
    ]
    return jnp.swapaxes(jnp.stack(parts), 0, 1).astype(BF16)


def some_rows_kernel(far, fields, chol, *outs):
    value = block_potential(fields[...], chol[...])
    size = value.shape[0] // far
    for k in range(far):
        outs[k][...] = value[k * size : (k + 1) * size]


def some_rows(fields, cholesky, far, block):
    slots, vectors = fields.shape
    columns = cholesky.shape[2]
    lanes = min(LANES, columns)
    size = slots // far
    return pl.pallas_call(
        functools.partial(some_rows_kernel, far),
        grid=(columns // lanes,),
        in_specs=[
            pl.BlockSpec((slots, vectors), lambda t: (0, 0)),
            pl.BlockSpec((vectors, ROWS, lanes), lambda t: (0, block, t)),
        ],
        out_specs=[pl.BlockSpec((size, ROWS, lanes), lambda t: (0, 0, t))] * far,
        out_shape=[jax.ShapeDtypeStruct((size, ROWS, columns), BF16)] * far,
        compiler_params=pltpu.CompilerParams(vmem_limit_bytes=48 << 20),
        cost_estimate=pl.CostEstimate(
            flops=2 * slots * vectors * ROWS * columns,
            bytes_accessed=2 * vectors * ROWS * columns,
            transcendentals=0,
        ),
    )(fields, cholesky)


def other_rows_kernel(near, far, cuts, fields, chol, *outs):
    value = block_potential(fields[...], chol[...])
    each = value.shape[0] // (near * far)
    for g, (low, high) in enumerate(cuts):
        for m in range(near):
            for k in range(far):
                at = (k * near + m) * each
                outs[g * near + m][k] = value[at + low : at + high]


def other_rows(fields, cholesky, near, far, cuts, done):
    slots, vectors = fields.shape
    rows, columns = cholesky.shape[1:]
    lanes = min(LANES, columns)
    shapes = [(far, high - low, ROWS) for low, high in cuts for _ in range(near)]
    return pl.pallas_call(
        functools.partial(other_rows_kernel, near, far, cuts),
        grid=(rows // ROWS - done, columns // lanes),
        in_specs=[
            pl.BlockSpec((slots, vectors), lambda r, t: (0, 0)),
            pl.BlockSpec((vectors, ROWS, lanes), lambda r, t: (0, r + done, t)),
        ],
        out_specs=[
            pl.BlockSpec(shape + (lanes,), lambda r, t: (0, 0, r, t)) for shape in shapes
        ],
        out_shape=[
            jax.ShapeDtypeStruct(shape[:2] + (rows - done * ROWS, columns), BF16)
            for shape in shapes
        ],
        compiler_params=pltpu.CompilerParams(vmem_limit_bytes=48 << 20),
        cost_estimate=pl.CostEstimate(
            flops=2 * slots * vectors * (rows - done * ROWS) * columns,
            bytes_accessed=2 * vectors * (rows - done * ROWS) * columns,
            transcendentals=0,
        ),
    )(fields, cholesky)


def taylor_kernel(near, far, tops, has_rest, me_ref, *refs):
    at = tops * near
    first = [refs[i * near : (i + 1) * near] for i in range(tops)]
    rest = refs[at : at + far] if has_rest else None
    at += far if has_rest else 0
    start = refs[at : at + near]
    outs = refs[at + near : at + 2 * near]
    terms = refs[at + 2 * near :]
    me = me_ref[0]
    group = len(terms)
    rows, electrons = terms[0].shape[1:]
    columns = first[0][0].shape[-1]
    order = [(k, m) for k in range(far) for m in range(near)]
    spans = [(i * ROWS, (i + 1) * ROWS) for i in range(tops)]
    if has_rest:
        spans.append((tops * ROWS, rows))

    def joined(pieces):
        wide = [piece.astype(F32) for piece in pieces]
        return jnp.concatenate(wide, axis=0).astype(BF16)

    matrices = []
    totals = []
    for w in range(group):
        blocks = [joined([part[m][k, w] for k, m in order]) for part in first]
        if has_rest:
            blocks.append(joined([rest[k][m, w] for k, m in order]))
        matrices.append(blocks)
        values = []
        for k, m in order:
            side = (w % 2) * electrons
            value = start[m][k, w // 2, :, side : side + electrons].astype(F32)
            terms[w][me ^ (k * near + m)] = value
            values.append(value)
        totals.append(
            [
                jnp.concatenate([value[low:high] for value in values], axis=0)
                for low, high in spans
            ]
        )
    for step in range(1, TERMS):
        for w in range(group):
            vector = terms[w][...].reshape(columns, electrons).astype(BF16)
            for part, (low, high) in enumerate(spans):
                size = high - low
                value = jnp.dot(matrices[w][part], vector, preferred_element_type=F32)
                value = (value * F32(1.0 / step)).astype(BF16).astype(F32)
                totals[w][part] = totals[w][part] + value
                if step + 1 < TERMS:
                    for i, (k, m) in enumerate(order):
                        terms[w][me ^ (k * near + m), low:high] = value[
                            i * size : (i + 1) * size
                        ]
    for i, (k, m) in enumerate(order):
        pieces = []
        for w in range(group):
            piece = [
                totals[w][part][i * (high - low) : (i + 1) * (high - low)]
                for part, (low, high) in enumerate(spans)
            ]
            pieces.append(jnp.concatenate(piece, axis=0))
        for w in range(0, group, 2):
            outs[m][k, w // 2] = jnp.concatenate(pieces[w : w + 2], axis=1).astype(BF16)


def taylor(me, first, rest, start, low, high):
    near = len(start)
    far = start[0].shape[0]
    columns = first[0][0].shape[3]
    rows = start[0].shape[2]
    electrons = start[0].shape[3] // 2
    pairs = (high - low) // 2
    group = high - low if high - low <= 4 and low % (high - low) == 0 else 2
    half = group // 2
    in_specs = [
        pl.BlockSpec(
            (far, group, ROWS, columns), lambda i, me: (0, low // group + i, 0, 0)
        )
    ] * (near * len(first))
    args = [block for part in first for block in part]
    if rest is not None:
        in_specs += [
            pl.BlockSpec((near, group) + rest[0].shape[2:], lambda i, me: (0, i, 0, 0))
        ] * far
        args += list(rest)
    in_specs += [
        pl.BlockSpec(
            (far, half, rows, 2 * electrons), lambda i, me: (0, low // group + i, 0, 0)
        )
    ] * near
    args += list(start)
    return pl.pallas_call(
        functools.partial(taylor_kernel, near, far, len(first), rest is not None),
        grid_spec=pltpu.PrefetchScalarGridSpec(
            num_scalar_prefetch=1,
            grid=((high - low) // group,),
            in_specs=in_specs,
            out_specs=[
                pl.BlockSpec((far, half, rows, 2 * electrons), lambda i, me: (0, i, 0, 0))
            ]
            * near,
            scratch_shapes=[pltpu.VMEM((near * far, rows, electrons), F32)] * group,
        ),
        out_shape=[jax.ShapeDtypeStruct((far, pairs, rows, 2 * electrons), BF16)] * near,
        compiler_params=pltpu.CompilerParams(vmem_limit_bytes=40 << 20),
        cost_estimate=pl.CostEstimate(
            flops=20 * pairs * columns * columns * electrons,
            bytes_accessed=4 * pairs * columns * columns,
            transcendentals=0,
        ),
    )(me[None], *args)


def far_hops(blocks, near):
    return [blocks[0]] + [hop(blocks[k], k * near) for k in range(1, len(blocks))]


def near_hops(blocks):
    return [blocks[0]] + [hop(blocks[m], m) for m in range(1, len(blocks))]


def far_then_near(blocks, near, far):
    got = far_hops(blocks, near)
    joined = [jnp.stack([got[k][m] for k in range(far)]) for m in range(near)]
    return near_hops(joined)


def near_then_far(blocks, near, far):
    got = near_hops(blocks)
    joined = [jnp.stack([got[m][k] for m in range(near)]) for k in range(far)]
    return far_hops(joined, near)


def local(walkers, cholesky, rotated, field_noise, sources):
    count, rows, electrons = walkers.shape
    vectors, _, columns = cholesky.shape
    slots = sources.shape[0]
    devices = lax.axis_size("orb")
    near = 4
    far = devices // near
    each = count // devices
    me = lax.axis_index("orb")
    column = me % near
    chunk = vectors // near

    partial = lax.dot_general(
        walkers.reshape(count, rows * electrons),
        rotated.reshape(vectors, rows * electrons),
        (((1,), (1,)), ((), ())),
        preferred_element_type=F32,
    ).astype(BF16)

    def own(m):
        return lax.dynamic_slice_in_dim(partial, (column ^ m) * chunk, chunk, 1)

    bias = sum(part.astype(F32) for part in near_hops([own(m) for m in range(near)]))
    shift = near
    while shift < devices:
        bias = bias.astype(BF16)
        bias = bias.astype(F32) + hop(bias, shift).astype(F32)
        shift *= 2
    parts = jnp.stack(near_hops([bias.astype(BF16)] * near))
    bias = jnp.concatenate(
        [
            lax.dynamic_index_in_dim(parts, column ^ c, 0, keepdims=False)
            for c in range(near)
        ],
        axis=1,
    )

    is_live = sources >= 0
    position = jnp.cumsum(is_live.astype(jnp.int32)) - 1
    row_index = jnp.arange(count, dtype=jnp.int32)
    wanted = ((row_index // each) ^ me) * each + row_index % each
    place = ((position[None, :] == wanted[:, None]) & is_live[None, :]).astype(BF16)
    named = (sources[:, None] == jnp.arange(count, dtype=jnp.int32)[None, :]).astype(BF16)
    select = jnp.dot(place, named, preferred_element_type=F32).astype(BF16)
    noise = jnp.dot(place, field_noise, preferred_element_type=F32)

    start = jnp.dot(
        select, walkers.reshape(count, rows * electrons), preferred_element_type=F32
    ).astype(BF16)
    start = start.reshape(far, near, each // 2, 2, rows, electrons)
    start = start.transpose(0, 1, 2, 4, 3, 5)
    start = start.reshape(far, near, each // 2, rows, 2 * electrons)
    start = far_then_near([start[k] for k in range(far)], near, far)

    picked = jnp.dot(select, bias, preferred_element_type=F32)
    fields = noise + picked
    weight = jnp.sum(fields * picked - 0.5 * picked * picked, axis=1)
    log_weight = jnp.sum(place.astype(F32) * weight[:, None], axis=0)
    fields = fields.astype(BF16)

    shape = (near, each, ROWS, columns)
    tops = min(2, rows // ROWS)
    first = []
    for i in range(tops):
        part = some_rows(fields, cholesky, far, i)
        part = [block.reshape(shape) for block in part]
        first.append(far_then_near(part, near, far))
    blocks = None
    cuts = [(0, each)]
    if rows > tops * ROWS:
        cuts = [(0, each // 2), (each // 2, each)]
        blocks = other_rows(fields, cholesky, near, far, cuts, tops)
    results = []
    for g, (low, high) in enumerate(cuts):
        rest = None
        if blocks is not None:
            mine = blocks[g * near : (g + 1) * near]
            rest = near_then_far(mine, near, far)
        grown = taylor(me, first, rest, start, low, high)
        back = near_then_far(grown, near, far)
        results.append(jnp.stack(back))
    grown = jnp.concatenate(results, axis=2)
    grown = grown.reshape(count // 2, rows, 2, electrons)
    new_walkers = jnp.einsum(
        "xipe,xps->sie", grown, place.reshape(count // 2, 2, slots),
        preferred_element_type=F32,
    ).astype(BF16)
    return (new_walkers, log_weight)


def solution(mesh):
    placed = (
        P("groups", "orb", None),
        P("groups", "orb", None),
        P("groups", "orb", None),
        P("groups", None),
        P("groups"),
    )


    return jax.shard_map(
        local,
        mesh=mesh,
        in_specs=placed,
        out_specs=(P("groups", "orb", None), P("groups")),
        check_vma=False,
    )
```

profile of v0, /device:TPU:0, one launch (start us, length us, event | category | flops | bytes accessed | tf_op | source)
XLA Modules:
  0.0 217.7 jit_solution(2465199273147761530)
XLA Ops:
  1.7 2.9 %fusion = bf16[128,1024]{1,0:T(8,128)(2,1)S(1)} fusion(bf16[128,32,64]{0,2,1:T(8,128)(2,1)S(1)} %copy-done, bf16[1024,32,64]{0,2,1:T(8,128)(2,1)} %param.7), kind=kOutput, calls=%fused_computation.4 | convolution fusion | flops 537001984 | bytes 4980736 | tf_op jit(solution)/shard_map/dot_general | solution.py:244
  5.2 2.6 %collective-permute-start.2 = (bf16[128,256]{1,0:T(8,128)(2,1)S(1)}, bf16[128,256]{1,0:T(8,128)(2,1)S(1)}, u32[]{:S(2)}, u32[]{:S(2)}) collective-permute-start(bf16[128,256]{1,0:T(8,128)(2,1)S(1)} %get-tuple-element.130), channel_id=1, source_target_pairs={{0,3},{1,2},{2,1},{3,0},{4,7},{5,6},{6,5},{7,4},{8,11},{9,10},{10,... | collective-permute-start | bytes 196616 | tf_op jit(solution)/shard_map/ppermute | solution.py:20
  12.3 3.1 %collective-permute-start.27 = (bf16[4,4,32,128]{3,2,1,0:T(8,128)(2,1)S(1)}, bf16[4,4,32,128]{3,2,1,0:T(8,128)(2,1)S(1)}, u32[]{:S(2)}, u32[]{:S(2)}) collective-permute-start(bf16[4,4,32,128]{3,2,1,0:T(8,128)(2,1)S(1)} %squeeze.28), channel_id=1, source_target_pairs={{0,8},{1,9},{2,10},{3,11},{4,12},{5,13},{6,14},{7,15},{8,0},{9,1},... | collective-permute-start | bytes 393224 | tf_op jit(solution)/shard_map/ppermute | solution.py:20
  20.0 8.3 %collective-permute-done.3 = bf16[128,256]{1,0:T(8,128)(2,1)S(1)} collective-permute-done((bf16[128,256]{1,0:T(8,128)(2,1)S(1)}, bf16[128,256]{1,0:T(8,128)(2,1)S(1)}, u32[]{:S(2)}, u32[]{:S(2)}) %collective-permute-start.3) | collective-permute-done | bytes 65568 | tf_op jit(solution)/shard_map/ppermute | solution.py:20
  31.5 2.8 %collective-permute-done.4 = bf16[128,256]{1,0:T(8,128)(2,1)S(1)} collective-permute-done((bf16[128,256]{1,0:T(8,128)(2,1)S(1)}, bf16[128,256]{1,0:T(8,128)(2,1)S(1)}, u32[]{:S(2)}, u32[]{:S(2)}) %collective-permute-start.4) | collective-permute-done | bytes 65568 | tf_op jit(solution)/shard_map/ppermute | solution.py:20
  36.3 2.4 %collective-permute-done.7 = bf16[128,256]{1,0:T(8,128)(2,1)S(1)} collective-permute-done((bf16[128,256]{1,0:T(8,128)(2,1)S(1)}, bf16[128,256]{1,0:T(8,128)(2,1)S(1)}, u32[]{:S(2)}, u32[]{:S(2)}) %collective-permute-start.7) | collective-permute-done | bytes 65568 | tf_op jit(solution)/shard_map/ppermute | solution.py:20
  40.9 5.5 %shard_map.69 = (bf16[32,8,512]{2,1,0:T(8,128)(2,1)S(1)}, bf16[32,8,512]{2,1,0:T(8,128)(2,1)S(1)}, bf16[32,8,512]{2,1,0:T(8,128)(2,1)S(1)}, bf16[32,8,512]{2,1,0:T(8,128)(2,1)S(1)}) custom-call(bf16[128,1024]{1,0:T(8,128)(2,1)S(1)} %get-tuple-element.60.fields, bf16[1024,32,512]{2,1,0:T(8,128)(2,1)} %chol.5), custom_call_target="tpu_custom_call" | custom-call | flops 1073741824 | bytes 8388608 | tf_op jit(solution)/shard_map/pallas_call | solution.py:43
  46.5 5.6 %shard_map.68 = (bf16[32,8,512]{2,1,0:T(8,128)(2,1)S(1)}, bf16[32,8,512]{2,1,0:T(8,128)(2,1)S(1)}, bf16[32,8,512]{2,1,0:T(8,128)(2,1)S(1)}, bf16[32,8,512]{2,1,0:T(8,128)(2,1)S(1)}) custom-call(bf16[128,1024]{1,0:T(8,128)(2,1)S(1)} %get-tuple-element.60.fields, bf16[1024,32,512]{2,1,0:T(8,128)(2,1)} %chol.5), custom_call_target="tpu_custom_call" | custom-call | flops 1073741824 | bytes 8388608 | tf_op jit(solution)/shard_map/pallas_call | solution.py:43
  52.0 9.8 %shard_map.70 = (bf16[4,4,16,512]{3,2,1,0:T(8,128)(2,1)S(1)}, bf16[4,4,16,512]{3,2,1,0:T(8,128)(2,1)S(1)}, bf16[4,4,16,512]{3,2,1,0:T(8,128)(2,1)S(1)}, bf16[4,4...) custom-call(bf16[128,1024]{1,0:T(8,128)(2,1)S(1)} %get-tuple-element, ...), custom_call_target="tpu_custom_call" | custom-call | flops 2147483648 | bytes 16777216 | tf_op jit(solution)/shard_map/pallas_call | solution.py:76
  67.1 7.7 %collective-permute-done.14 = bf16[4,8,8,512]{3,2,1,0:T(8,128)(2,1)S(1)} collective-permute-done((bf16[4,8,8,512]{3,2,1,0:T(8,128)(2,1)S(1)}, bf16[4,8,8,512]{3,2,1,0:T(8,128)(2,1)S(1)}, u32[]{:S(2)}, u32[]{:S(2)}) %collective-permute-start.14) | collective-permute-done | bytes 262176 | tf_op jit(solution)/shard_map/ppermute | solution.py:20
  74.9 9.4 %collective-permute-done.15 = bf16[4,8,8,512]{3,2,1,0:T(8,128)(2,1)S(1)} collective-permute-done((bf16[4,8,8,512]{3,2,1,0:T(8,128)(2,1)S(1)}, bf16[4,8,8,512]{3,2,1,0:T(8,128)(2,1)S(1)}, u32[]{:S(2)}, u32[]{:S(2)}) %collective-permute-start.15) | collective-permute-done | bytes 262176 | tf_op jit(solution)/shard_map/ppermute | solution.py:20
  86.0 3.1 %collective-permute-done.8 = bf16[4,8,8,512]{3,2,1,0:T(8,128)(2,1)S(1)} collective-permute-done((bf16[4,8,8,512]{3,2,1,0:T(8,128)(2,1)S(1)}, bf16[4,8,8,512]{3,2,1,0:T(8,128)(2,1)S(1)}, u32[]{:S(2)}, u32[]{:S(2)}) %collective-permute-start.8) | collective-permute-done | bytes 262176 | tf_op jit(solution)/shard_map/ppermute | solution.py:20
  89.1 17.6 %collective-permute-done.9 = bf16[4,8,8,512]{3,2,1,0:T(8,128)(2,1)S(1)} collective-permute-done((bf16[4,8,8,512]{3,2,1,0:T(8,128)(2,1)S(1)}, bf16[4,8,8,512]{3,2,1,0:T(8,128)(2,1)S(1)}, u32[]{:S(2)}, u32[]{:S(2)}) %collective-permute-start.9) | collective-permute-done | bytes 262176 | tf_op jit(solution)/shard_map/ppermute | solution.py:20
  109.1 5.8 %collective-permute-done.21 = bf16[4,4,16,512]{3,2,1,0:T(8,128)(2,1)S(1)} collective-permute-done((bf16[4,4,16,512]{3,2,1,0:T(8,128)(2,1)S(1)}, bf16[4,4,16,512]{3,2,1,0:T(8,128)(2,1)S(1)}, u32[]{:S(2)}, u32[]{:S(2)}) %collective-permute-start.21) | collective-permute-done | bytes 262176 | tf_op jit(solution)/shard_map/ppermute | solution.py:20
  114.9 2.5 %collective-permute-start.39 = (bf16[4,4,16,512]{3,2,1,0:T(8,128)(2,1)S(1)}, bf16[4,4,16,512]{3,2,1,0:T(8,128)(2,1)S(1)}, u32[]{:S(2)}, u32[]{:S(2)}) collective-permute-start(bf16[4,4,16,512]{3,2,1,0:T(8,128)(2,1)S(1)} %get-tuple-element.44), channel_id=1, source_target_pairs={{0,2},{1,3},{2,0},{3,1},{4,6},{5,7},{6,4},{7,5},{8,10},{9,11},{10,... | collective-permute-start | bytes 786440 | tf_op jit(solution)/shard_map/ppermute | solution.py:20
  117.5 3.0 %collective-permute-done.22 = bf16[4,4,16,512]{3,2,1,0:T(8,128)(2,1)S(1)} collective-permute-done((bf16[4,4,16,512]{3,2,1,0:T(8,128)(2,1)S(1)}, bf16[4,4,16,512]{3,2,1,0:T(8,128)(2,1)S(1)}, u32[]{:S(2)}, u32[]{:S(2)}) %collective-permute-start.22) | collective-permute-done | bytes 262176 | tf_op jit(solution)/shard_map/ppermute | solution.py:20
  122.7 3.3 %collective-permute-done.39 = bf16[4,4,16,512]{3,2,1,0:T(8,128)(2,1)S(1)} collective-permute-done((bf16[4,4,16,512]{3,2,1,0:T(8,128)(2,1)S(1)}, bf16[4,4,16,512]{3,2,1,0:T(8,128)(2,1)S(1)}, u32[]{:S(2)}, u32[]{:S(2)}) %collective-permute-start.39) | collective-permute-done | bytes 262176 | tf_op jit(solution)/shard_map/ppermute | solution.py:20
  126.0 2.5 %collective-permute-start.18 = (bf16[4,8,8,512]{3,2,1,0:T(8,128)(2,1)S(1)}, bf16[4,8,8,512]{3,2,1,0:T(8,128)(2,1)S(1)}, u32[]{:S(2)}, u32[]{:S(2)}) collective-permute-start(bf16[4,8,8,512]{3,2,1,0:T(8,128)(2,1)S(1)} %pad_maximum_fusion.7), channel_id=1, source_target_pairs={{0,2},{1,3},{2,0},{3,1},{4,6},{5,7},{6,4},{7,5},{8,10},{9,11},{10,... | collective-permute-start | bytes 786440 | tf_op jit(solution)/shard_map/ppermute | solution.py:20
  128.5 3.1 %collective-permute-done.40 = bf16[4,4,16,512]{3,2,1,0:T(8,128)(2,1)S(1)} collective-permute-done((bf16[4,4,16,512]{3,2,1,0:T(8,128)(2,1)S(1)}, bf16[4,4,16,512]{3,2,1,0:T(8,128)(2,1)S(1)}, u32[]{:S(2)}, u32[]{:S(2)}) %collective-permute-start.40) | collective-permute-done | bytes 262176 | tf_op jit(solution)/shard_map/ppermute | solution.py:20
  134.0 9.4 %collective-permute-done.31.refs_15_ = bf16[4,4,32,128]{3,2,1,0:T(8,128)(2,1)S(1)} collective-permute-done((bf16[4,4,32,128]{3,2,1,0:T(8,128)(2,1)S(1)}, bf16[4,4,32,128]{3,2,1,0:T(8,128)(2,1)S(1)}, u32[]{:S(2)}, u32[]{:S(2)}) %collective-permute-start.31) | collective-permute-done | bytes 131104 | tf_op jit(solution)/shard_map/ppermute | solution.py:20
  149.7 2.8 %collective-permute-done.12.refs_2_ = bf16[4,8,8,512]{3,2,1,0:T(8,128)(2,1)S(1)} collective-permute-done((bf16[4,8,8,512]{3,2,1,0:T(8,128)(2,1)S(1)}, bf16[4,8,8,512]{3,2,1,0:T(8,128)(2,1)S(1)}, u32[]{:S(2)}, u32[]{:S(2)}) %collective-permute-start.12) | collective-permute-done | bytes 262176 | tf_op jit(solution)/shard_map/ppermute | solution.py:20
  154.3 2.8 %collective-permute-done.13.refs_3_ = bf16[4,8,8,512]{3,2,1,0:T(8,128)(2,1)S(1)} collective-permute-done((bf16[4,8,8,512]{3,2,1,0:T(8,128)(2,1)S(1)}, bf16[4,8,8,512]{3,2,1,0:T(8,128)(2,1)S(1)}, u32[]{:S(2)}, u32[]{:S(2)}) %collective-permute-start.13) | collective-permute-done | bytes 262176 | tf_op jit(solution)/shard_map/ppermute | solution.py:20
  159.1 2.1 collective-permute-start.43
  161.2 6.8 %collective-permute-done.24.refs_10_ = bf16[4,4,16,512]{3,2,1,0:T(8,128)(2,1)S(1)} collective-permute-done((bf16[4,4,16,512]{3,2,1,0:T(8,128)(2,1)S(1)}, bf16[4,4,16,512]{3,2,1,0:T(8,128)(2,1)S(1)}, u32[]{:S(2)}, u32[]{:S(2)}) %collective-permute-start.24) | collective-permute-done | bytes 262176 | tf_op jit(solution)/shard_map/ppermute | solution.py:20
  168.0 3.1 %shard_map.71 = (bf16[4,2,32,128]{3,2,1,0:T(8,128)(2,1)S(1)}, bf16[4,2,32,128]{3,2,1,0:T(8,128)(2,1)S(1)}, bf16[4,2,32,128]{3,2,1,0:T(8,128)(2,1)S(1)}, bf16[4,2,32,128]{3,2,1,0:T(8,128)(2,1)S(1)}) custom-call(s32[1]{0:T(128)} %bitcast.3.me_ref, bf16[4,8,8,512]{3,2,1,0:T(8,128)(2,1)S(1)} %get-tuple-element.181.refs_0_, ...), custom_call_target="tpu_custom_call" | custom-call | flops 671088640 | bytes 2097152 | tf_op jit(solution)/shard_map/pallas_call | solution.py:190
  173.1 17.4 %collective-permute-done.42.refs_10_ = bf16[4,4,16,512]{3,2,1,0:T(8,128)(2,1)S(1)} collective-permute-done((bf16[4,4,16,512]{3,2,1,0:T(8,128)(2,1)S(1)}, bf16[4,4,16,512]{3,2,1,0:T(8,128)(2,1)S(1)}, u32[]{:S(2)}, u32[]{:S(2)}) %collective-permute-start.42) | collective-permute-done | bytes 262176 | tf_op jit(solution)/shard_map/ppermute | solution.py:20
  190.5 3.1 %shard_map.72 = (bf16[4,2,32,128]{3,2,1,0:T(8,128)(2,1)S(1)}, bf16[4,2,32,128]{3,2,1,0:T(8,128)(2,1)S(1)}, bf16[4,2,32,128]{3,2,1,0:T(8,128)(2,1)S(1)}, bf16[4,2,32,128]{3,2,1,0:T(8,128)(2,1)S(1)}) custom-call(s32[1]{0:T(128)} %bitcast.3.me_ref, bf16[4,8,8,512]{3,2,1,0:T(8,128)(2,1)S(1)} %get-tuple-element.181.refs_0_, ...), custom_call_target="tpu_custom_call" | custom-call | flops 671088640 | bytes 2097152 | tf_op jit(solution)/shard_map/pallas_call | solution.py:190
  195.6 5.7 %collective-permute-start.35 = (bf16[4,2,32,128]{3,2,1,0:T(8,128)(2,1)S(1)}, bf16[4,2,32,128]{3,2,1,0:T(8,128)(2,1)S(1)}, u32[]{:S(2)}, u32[]{:S(2)}) collective-permute-start(bf16[4,2,32,128]{3,2,1,0:T(8,128)(2,1)S(1)} %pad_maximum_fusion.21), channel_id=1, source_target_pairs={{0,4},{1,5},{2,6},{3,7},{4,0},{5,1},{6,2},{7,3},{8,12},{9,13},{10,... | collective-permute-start | bytes 196616 | tf_op jit(solution)/shard_map/ppermute | solution.py:20
  201.7 2.2 collective-permute-start.37
  206.4 2.2 collective-permute-start.49
  210.0 5.2 %collective-permute-done.48 = bf16[4,2,32,128]{3,2,1,0:T(8,128)(2,1)S(1)} collective-permute-done((bf16[4,2,32,128]{3,2,1,0:T(8,128)(2,1)S(1)}, bf16[4,2,32,128]{3,2,1,0:T(8,128)(2,1)S(1)}, u32[]{:S(2)}, u32[]{:S(2)}) %collective-permute-start.48) | collective-permute-done | bytes 65568 | tf_op jit(solution)/shard_map/ppermute | solution.py:20
  215.6 2.1 bitcast_convert_fusion
  (168 shorter events, 50.6 us)
Async XLA Ops:
  4.7 13.1 %collective-permute-start = (bf16[128,256]{1,0:T(8,128)(2,1)S(1)}, bf16[128,256]{1,0:T(8,128)(2,1)S(1)}, u32[]{:S(2)}, u32[]{:S(2)}) collective-permute-start(bf16[128,256]{1,0:T(8,128)(2,1)S(1)} %get-tuple-element.129), channel_id=1, source_target_pairs={{0,1},{1,0},{2,3},{3,2},{4,5},{5,4},{6,7},{7,6},{8,9},{9,8},{10,11... | collective-permute-start | bytes 196616 | tf_op jit(solution)/shard_map/ppermute | solution.py:20
  5.2 12.9 %collective-permute-start.2 = (bf16[128,256]{1,0:T(8,128)(2,1)S(1)}, bf16[128,256]{1,0:T(8,128)(2,1)S(1)}, u32[]{:S(2)}, u32[]{:S(2)}) collective-permute-start(bf16[128,256]{1,0:T(8,128)(2,1)S(1)} %get-tuple-element.130), channel_id=1, source_target_pairs={{0,3},{1,2},{2,1},{3,0},{4,7},{5,6},{6,5},{7,4},{8,11},{9,10},{10,... | collective-permute-start | bytes 196616 | tf_op jit(solution)/shard_map/ppermute | solution.py:20
  12.3 17.4 %collective-permute-start.27 = (bf16[4,4,32,128]{3,2,1,0:T(8,128)(2,1)S(1)}, bf16[4,4,32,128]{3,2,1,0:T(8,128)(2,1)S(1)}, u32[]{:S(2)}, u32[]{:S(2)}) collective-permute-start(bf16[4,4,32,128]{3,2,1,0:T(8,128)(2,1)S(1)} %squeeze.28), channel_id=1, source_target_pairs={{0,8},{1,9},{2,10},{3,11},{4,12},{5,13},{6,14},{7,15},{8,0},{9,1},... | collective-permute-start | bytes 393224 | tf_op jit(solution)/shard_map/ppermute | solution.py:20
  15.6 14.1 %collective-permute-start.28 = (bf16[4,4,32,128]{3,2,1,0:T(8,128)(2,1)S(1)}, bf16[4,4,32,128]{3,2,1,0:T(8,128)(2,1)S(1)}, u32[]{:S(2)}, u32[]{:S(2)}) collective-permute-start(bf16[4,4,32,128]{3,2,1,0:T(8,128)(2,1)S(1)} %squeeze.29), channel_id=1, source_target_pairs={{0,12},{1,13},{2,14},{3,15},{4,8},{5,9},{6,10},{7,11},{8,4},{9,5},... | collective-permute-start | bytes 393224 | tf_op jit(solution)/shard_map/ppermute | solution.py:20
  17.8 11.9 %collective-permute-start.26 = (bf16[4,4,32,128]{3,2,1,0:T(8,128)(2,1)S(1)}, bf16[4,4,32,128]{3,2,1,0:T(8,128)(2,1)S(1)}, u32[]{:S(2)}, u32[]{:S(2)}) collective-permute-start(bf16[4,4,32,128]{3,2,1,0:T(8,128)(2,1)S(1)} %squeeze.27), channel_id=1, source_target_pairs={{0,4},{1,5},{2,6},{3,7},{4,0},{5,1},{6,2},{7,3},{8,12},{9,13},{10,... | collective-permute-start | bytes 393224 | tf_op jit(solution)/shard_map/ppermute | solution.py:20
  29.8 103.9 %collective-permute-start.29 = (bf16[4,4,32,128]{3,2,1,0:T(8,128)(2,1)S(1)}, bf16[4,4,32,128]{3,2,1,0:T(8,128)(2,1)S(1)}, u32[]{:S(2)}, u32[]{:S(2)}) collective-permute-start(bf16[4,4,32,128]{3,2,1,0:T(8,128)(2,1)S(1)} %pad_maximum_fusion.18), channel_id=1, source_target_pairs={{0,1},{1,0},{2,3},{3,2},{4,5},{5,4},{6,7},{7,6},{8,9},{9,8},{10,11... | collective-permute-start | bytes 393224 | tf_op jit(solution)/shard_map/ppermute | solution.py:20
  29.9 103.9 %collective-permute-start.30 = (bf16[4,4,32,128]{3,2,1,0:T(8,128)(2,1)S(1)}, bf16[4,4,32,128]{3,2,1,0:T(8,128)(2,1)S(1)}, u32[]{:S(2)}, u32[]{:S(2)}) collective-permute-start(bf16[4,4,32,128]{3,2,1,0:T(8,128)(2,1)S(1)} %pad_maximum_fusion.19), channel_id=1, source_target_pairs={{0,2},{1,3},{2,0},{3,1},{4,6},{5,7},{6,4},{7,5},{8,10},{9,11},{10,... | collective-permute-start | bytes 393224 | tf_op jit(solution)/shard_map/ppermute | solution.py:20
  61.9 12.9 %collective-permute-start.14 = (bf16[4,8,8,512]{3,2,1,0:T(8,128)(2,1)S(1)}, bf16[4,8,8,512]{3,2,1,0:T(8,128)(2,1)S(1)}, u32[]{:S(2)}, u32[]{:S(2)}) collective-permute-start(bf16[4,8,8,512]{3,2,1,0:T(8,128)(2,1)S(1)} %bitcast.77), channel_id=1, source_target_pairs={{0,4},{1,5},{2,6},{3,7},{4,0},{5,1},{6,2},{7,3},{8,12},{9,13},{10,... | collective-permute-start | bytes 786440 | tf_op jit(solution)/shard_map/ppermute | solution.py:20
  62.9 21.4 %collective-permute-start.15 = (bf16[4,8,8,512]{3,2,1,0:T(8,128)(2,1)S(1)}, bf16[4,8,8,512]{3,2,1,0:T(8,128)(2,1)S(1)}, u32[]{:S(2)}, u32[]{:S(2)}) collective-permute-start(bf16[4,8,8,512]{3,2,1,0:T(8,128)(2,1)S(1)} %bitcast.76), channel_id=1, source_target_pairs={{0,8},{1,9},{2,10},{3,11},{4,12},{5,13},{6,14},{7,15},{8,0},{9,1},... | collective-permute-start | bytes 786440 | tf_op jit(solution)/shard_map/ppermute | solution.py:20
  65.7 18.6 %collective-permute-start.16 = (bf16[4,8,8,512]{3,2,1,0:T(8,128)(2,1)S(1)}, bf16[4,8,8,512]{3,2,1,0:T(8,128)(2,1)S(1)}, u32[]{:S(2)}, u32[]{:S(2)}) collective-permute-start(bf16[4,8,8,512]{3,2,1,0:T(8,128)(2,1)S(1)} %bitcast.75), channel_id=1, source_target_pairs={{0,12},{1,13},{2,14},{3,15},{4,8},{5,9},{6,10},{7,11},{8,4},{9,5},... | collective-permute-start | bytes 786440 | tf_op jit(solution)/shard_map/ppermute | solution.py:20
  74.8 14.3 %collective-permute-start.8 = (bf16[4,8,8,512]{3,2,1,0:T(8,128)(2,1)S(1)}, bf16[4,8,8,512]{3,2,1,0:T(8,128)(2,1)S(1)}, u32[]{:S(2)}, u32[]{:S(2)}) collective-permute-start(bf16[4,8,8,512]{3,2,1,0:T(8,128)(2,1)S(1)} %bitcast.74), channel_id=1, source_target_pairs={{0,4},{1,5},{2,6},{3,7},{4,0},{5,1},{6,2},{7,3},{8,12},{9,13},{10,... | collective-permute-start | bytes 786440 | tf_op jit(solution)/shard_map/ppermute | solution.py:20
  84.2 22.5 %collective-permute-start.9 = (bf16[4,8,8,512]{3,2,1,0:T(8,128)(2,1)S(1)}, bf16[4,8,8,512]{3,2,1,0:T(8,128)(2,1)S(1)}, u32[]{:S(2)}, u32[]{:S(2)}) collective-permute-start(bf16[4,8,8,512]{3,2,1,0:T(8,128)(2,1)S(1)} %bitcast.73), channel_id=1, source_target_pairs={{0,8},{1,9},{2,10},{3,11},{4,12},{5,13},{6,14},{7,15},{8,0},{9,1},... | collective-permute-start | bytes 786440 | tf_op jit(solution)/shard_map/ppermute | solution.py:20
  84.3 24.0 %collective-permute-start.10 = (bf16[4,8,8,512]{3,2,1,0:T(8,128)(2,1)S(1)}, bf16[4,8,8,512]{3,2,1,0:T(8,128)(2,1)S(1)}, u32[]{:S(2)}, u32[]{:S(2)}) collective-permute-start(bf16[4,8,8,512]{3,2,1,0:T(8,128)(2,1)S(1)} %bitcast.72), channel_id=1, source_target_pairs={{0,12},{1,13},{2,14},{3,15},{4,8},{5,9},{6,10},{7,11},{8,4},{9,5},... | collective-permute-start | bytes 786440 | tf_op jit(solution)/shard_map/ppermute | solution.py:20
  89.1 19.3 %collective-permute-start.20 = (bf16[4,4,16,512]{3,2,1,0:T(8,128)(2,1)S(1)}, bf16[4,4,16,512]{3,2,1,0:T(8,128)(2,1)S(1)}, u32[]{:S(2)}, u32[]{:S(2)}) collective-permute-start(bf16[4,4,16,512]{3,2,1,0:T(8,128)(2,1)S(1)} %get-tuple-element.35), channel_id=1, source_target_pairs={{0,1},{1,0},{2,3},{3,2},{4,5},{5,4},{6,7},{7,6},{8,9},{9,8},{10,11... | collective-permute-start | bytes 786440 | tf_op jit(solution)/shard_map/ppermute | solution.py:20
  108.3 12.3 %collective-permute-start.22 = (bf16[4,4,16,512]{3,2,1,0:T(8,128)(2,1)S(1)}, bf16[4,4,16,512]{3,2,1,0:T(8,128)(2,1)S(1)}, u32[]{:S(2)}, u32[]{:S(2)}) collective-permute-start(bf16[4,4,16,512]{3,2,1,0:T(8,128)(2,1)S(1)} %get-tuple-element.37), channel_id=1, source_target_pairs={{0,3},{1,2},{2,1},{3,0},{4,7},{5,6},{6,5},{7,4},{8,11},{9,10},{10,... | collective-permute-start | bytes 786440 | tf_op jit(solution)/shard_map/ppermute | solution.py:20
  108.4 14.0 %collective-permute-start.38 = (bf16[4,4,16,512]{3,2,1,0:T(8,128)(2,1)S(1)}, bf16[4,4,16,512]{3,2,1,0:T(8,128)(2,1)S(1)}, u32[]{:S(2)}, u32[]{:S(2)}) collective-permute-start(bf16[4,4,16,512]{3,2,1,0:T(8,128)(2,1)S(1)} %get-tuple-element.43), channel_id=1, source_target_pairs={{0,1},{1,0},{2,3},{3,2},{4,5},{5,4},{6,7},{7,6},{8,9},{9,8},{10,11... | collective-permute-start | bytes 786440 | tf_op jit(solution)/shard_map/ppermute | solution.py:20
  114.9 11.1 %collective-permute-start.39 = (bf16[4,4,16,512]{3,2,1,0:T(8,128)(2,1)S(1)}, bf16[4,4,16,512]{3,2,1,0:T(8,128)(2,1)S(1)}, u32[]{:S(2)}, u32[]{:S(2)}) collective-permute-start(bf16[4,4,16,512]{3,2,1,0:T(8,128)(2,1)S(1)} %get-tuple-element.44), channel_id=1, source_target_pairs={{0,2},{1,3},{2,0},{3,1},{4,6},{5,7},{6,4},{7,5},{8,10},{9,11},{10,... | collective-permute-start | bytes 786440 | tf_op jit(solution)/shard_map/ppermute | solution.py:20
  120.5 11.1 %collective-permute-start.40 = (bf16[4,4,16,512]{3,2,1,0:T(8,128)(2,1)S(1)}, bf16[4,4,16,512]{3,2,1,0:T(8,128)(2,1)S(1)}, u32[]{:S(2)}, u32[]{:S(2)}) collective-permute-start(bf16[4,4,16,512]{3,2,1,0:T(8,128)(2,1)S(1)} %get-tuple-element.45), channel_id=1, source_target_pairs={{0,3},{1,2},{2,1},{3,0},{4,7},{5,6},{6,5},{7,4},{8,11},{9,10},{10,... | collective-permute-start | bytes 786440 | tf_op jit(solution)/shard_map/ppermute | solution.py:20
  122.4 21.1 %collective-permute-start.17 = (bf16[4,8,8,512]{3,2,1,0:T(8,128)(2,1)S(1)}, bf16[4,8,8,512]{3,2,1,0:T(8,128)(2,1)S(1)}, u32[]{:S(2)}, u32[]{:S(2)}) collective-permute-start(bf16[4,8,8,512]{3,2,1,0:T(8,128)(2,1)S(1)} %pad_maximum_fusion.6), channel_id=1, source_target_pairs={{0,1},{1,0},{2,3},{3,2},{4,5},{5,4},{6,7},{7,6},{8,9},{9,8},{10,11... | collective-permute-start | bytes 786440 | tf_op jit(solution)/shard_map/ppermute | solution.py:20
  126.0 19.1 %collective-permute-start.18 = (bf16[4,8,8,512]{3,2,1,0:T(8,128)(2,1)S(1)}, bf16[4,8,8,512]{3,2,1,0:T(8,128)(2,1)S(1)}, u32[]{:S(2)}, u32[]{:S(2)}) collective-permute-start(bf16[4,8,8,512]{3,2,1,0:T(8,128)(2,1)S(1)} %pad_maximum_fusion.7), channel_id=1, source_target_pairs={{0,2},{1,3},{2,0},{3,1},{4,6},{5,7},{6,4},{7,5},{8,10},{9,11},{10,... | collective-permute-start | bytes 786440 | tf_op jit(solution)/shard_map/ppermute | solution.py:20
  131.6 15.0 %collective-permute-start.19 = (bf16[4,8,8,512]{3,2,1,0:T(8,128)(2,1)S(1)}, bf16[4,8,8,512]{3,2,1,0:T(8,128)(2,1)S(1)}, u32[]{:S(2)}, u32[]{:S(2)}) collective-permute-start(bf16[4,8,8,512]{3,2,1,0:T(8,128)(2,1)S(1)} %pad_maximum_fusion.8), channel_id=1, source_target_pairs={{0,3},{1,2},{2,1},{3,0},{4,7},{5,6},{6,5},{7,4},{8,11},{9,10},{10,... | collective-permute-start | bytes 786440 | tf_op jit(solution)/shard_map/ppermute | solution.py:20
  133.7 13.8 %collective-permute-start.11 = (bf16[4,8,8,512]{3,2,1,0:T(8,128)(2,1)S(1)}, bf16[4,8,8,512]{3,2,1,0:T(8,128)(2,1)S(1)}, u32[]{:S(2)}, u32[]{:S(2)}) collective-permute-start(bf16[4,8,8,512]{3,2,1,0:T(8,128)(2,1)S(1)} %pad_maximum_fusion.2), channel_id=1, source_target_pairs={{0,1},{1,0},{2,3},{3,2},{4,5},{5,4},{6,7},{7,6},{8,9},{9,8},{10,11... | collective-permute-start | bytes 786440 | tf_op jit(solution)/shard_map/ppermute | solution.py:20
  143.5 13.6 %collective-permute-start.13 = (bf16[4,8,8,512]{3,2,1,0:T(8,128)(2,1)S(1)}, bf16[4,8,8,512]{3,2,1,0:T(8,128)(2,1)S(1)}, u32[]{:S(2)}, u32[]{:S(2)}) collective-permute-start(bf16[4,8,8,512]{3,2,1,0:T(8,128)(2,1)S(1)} %pad_maximum_fusion.4), channel_id=1, source_target_pairs={{0,3},{1,2},{2,1},{3,0},{4,7},{5,6},{6,5},{7,4},{8,11},{9,10},{10,... | collective-permute-start | bytes 786440 | tf_op jit(solution)/shard_map/ppermute | solution.py:20
  145.1 13.9 %collective-permute-start.23 = (bf16[4,4,16,512]{3,2,1,0:T(8,128)(2,1)S(1)}, bf16[4,4,16,512]{3,2,1,0:T(8,128)(2,1)S(1)}, u32[]{:S(2)}, u32[]{:S(2)}) collective-permute-start(bf16[4,4,16,512]{3,2,1,0:T(8,128)(2,1)S(1)} %pad_maximum_fusion.10), channel_id=1, source_target_pairs={{0,4},{1,5},{2,6},{3,7},{4,0},{5,1},{6,2},{7,3},{8,12},{9,13},{10,... | collective-permute-start | bytes 786440 | tf_op jit(solution)/shard_map/ppermute | solution.py:20
  146.6 21.4 %collective-permute-start.24 = (bf16[4,4,16,512]{3,2,1,0:T(8,128)(2,1)S(1)}, bf16[4,4,16,512]{3,2,1,0:T(8,128)(2,1)S(1)}, u32[]{:S(2)}, u32[]{:S(2)}) collective-permute-start(bf16[4,4,16,512]{3,2,1,0:T(8,128)(2,1)S(1)} %pad_maximum_fusion.11), channel_id=1, source_target_pairs={{0,8},{1,9},{2,10},{3,11},{4,12},{5,13},{6,14},{7,15},{8,0},{9,1},... | collective-permute-start | bytes 786440 | tf_op jit(solution)/shard_map/ppermute | solution.py:20
  147.5 20.6 %collective-permute-start.25 = (bf16[4,4,16,512]{3,2,1,0:T(8,128)(2,1)S(1)}, bf16[4,4,16,512]{3,2,1,0:T(8,128)(2,1)S(1)}, u32[]{:S(2)}, u32[]{:S(2)}) collective-permute-start(bf16[4,4,16,512]{3,2,1,0:T(8,128)(2,1)S(1)} %pad_maximum_fusion.12), channel_id=1, source_target_pairs={{0,12},{1,13},{2,14},{3,15},{4,8},{5,9},{6,10},{7,11},{8,4},{9,5},... | collective-permute-start | bytes 786440 | tf_op jit(solution)/shard_map/ppermute | solution.py:20
  152.5 19.4 %collective-permute-start.41 = (bf16[4,4,16,512]{3,2,1,0:T(8,128)(2,1)S(1)}, bf16[4,4,16,512]{3,2,1,0:T(8,128)(2,1)S(1)}, u32[]{:S(2)}, u32[]{:S(2)}) collective-permute-start(bf16[4,4,16,512]{3,2,1,0:T(8,128)(2,1)S(1)} %pad_maximum_fusion.14), channel_id=1, source_target_pairs={{0,4},{1,5},{2,6},{3,7},{4,0},{5,1},{6,2},{7,3},{8,12},{9,13},{10,... | collective-permute-start | bytes 786440 | tf_op jit(solution)/shard_map/ppermute | solution.py:20
  157.1 33.4 %collective-permute-start.42 = (bf16[4,4,16,512]{3,2,1,0:T(8,128)(2,1)S(1)}, bf16[4,4,16,512]{3,2,1,0:T(8,128)(2,1)S(1)}, u32[]{:S(2)}, u32[]{:S(2)}) collective-permute-start(bf16[4,4,16,512]{3,2,1,0:T(8,128)(2,1)S(1)} %pad_maximum_fusion.15), channel_id=1, source_target_pairs={{0,8},{1,9},{2,10},{3,11},{4,12},{5,13},{6,14},{7,15},{8,0},{9,1},... | collective-permute-start | bytes 786440 | tf_op jit(solution)/shard_map/ppermute | solution.py:20
  159.1 31.4 %collective-permute-start.43 = (bf16[4,4,16,512]{3,2,1,0:T(8,128)(2,1)S(1)}, bf16[4,4,16,512]{3,2,1,0:T(8,128)(2,1)S(1)}, u32[]{:S(2)}, u32[]{:S(2)}) collective-permute-start(bf16[4,4,16,512]{3,2,1,0:T(8,128)(2,1)S(1)} %pad_maximum_fusion.16), channel_id=1, source_target_pairs={{0,12},{1,13},{2,14},{3,15},{4,8},{5,9},{6,10},{7,11},{8,4},{9,5},... | collective-permute-start | bytes 786440 | tf_op jit(solution)/shard_map/ppermute | solution.py:20
  171.1 23.3 %collective-permute-start.32 = (bf16[4,2,32,128]{3,2,1,0:T(8,128)(2,1)S(1)}, bf16[4,2,32,128]{3,2,1,0:T(8,128)(2,1)S(1)}, u32[]{:S(2)}, u32[]{:S(2)}) collective-permute-start(bf16[4,2,32,128]{3,2,1,0:T(8,128)(2,1)S(1)} %get-tuple-element.39), channel_id=1, source_target_pairs={{0,1},{1,0},{2,3},{3,2},{4,5},{5,4},{6,7},{7,6},{8,9},{9,8},{10,11... | collective-permute-start | bytes 196616 | tf_op jit(solution)/shard_map/ppermute | solution.py:20
  171.2 24.3 %collective-permute-start.33 = (bf16[4,2,32,128]{3,2,1,0:T(8,128)(2,1)S(1)}, bf16[4,2,32,128]{3,2,1,0:T(8,128)(2,1)S(1)}, u32[]{:S(2)}, u32[]{:S(2)}) collective-permute-start(bf16[4,2,32,128]{3,2,1,0:T(8,128)(2,1)S(1)} %get-tuple-element.40), channel_id=1, source_target_pairs={{0,2},{1,3},{2,0},{3,1},{4,6},{5,7},{6,4},{7,5},{8,10},{9,11},{10,... | collective-permute-start | bytes 196616 | tf_op jit(solution)/shard_map/ppermute | solution.py:20
  171.9 23.7 %collective-permute-start.34 = (bf16[4,2,32,128]{3,2,1,0:T(8,128)(2,1)S(1)}, bf16[4,2,32,128]{3,2,1,0:T(8,128)(2,1)S(1)}, u32[]{:S(2)}, u32[]{:S(2)}) collective-permute-start(bf16[4,2,32,128]{3,2,1,0:T(8,128)(2,1)S(1)} %get-tuple-element.41), channel_id=1, source_target_pairs={{0,3},{1,2},{2,1},{3,0},{4,7},{5,6},{6,5},{7,4},{8,11},{9,10},{10,... | collective-permute-start | bytes 196616 | tf_op jit(solution)/shard_map/ppermute | solution.py:20
  (22 other events, 212.6 us)
where the time goes:
time: 218 us
  waiting for transfers between devices  115 us (53%)
  starting transfers between devices  59.8 us (27%)
  Pallas kernels  27.1 us (12%)
  matrix products  6.16 us (3%)
  local copies, waits for them, and re-layouts  6.11 us (3%)
    ppermute x50, waiting for transfers between devices, hop(): return lax.ppermute(value, 'orb', [(i, i ^ mask) for i in range(size)])  115 us
    ppermute x50, starting transfers between devices, hop(): return lax.ppermute(value, 'orb', [(i, i ^ mask) for i in range(size)])  59.8 us
    pallas_call x2, Pallas kernels, some_rows(): pl.pallas_call(functools.partial(some_rows_kernel, far), grid=(columns //...  11.1 us
    pallas_call x1, Pallas kernels, other_rows(): pl.pallas_call(functools.partial(other_rows_kernel, near, far, cuts), gri...  9.85 us
    pallas_call x2, Pallas kernels, taylor(): pl.pallas_call(functools.partial(taylor_kernel, near, far, len(first), re...  6.16 us
  transfers between devices with their start and end apart: 50, of which 20 were waited for; matrix products, arithmetic and copies ran while one was open for 4% of the time, Pallas kernels for 12%

commit v1 on v0

--- a/solution.py
+++ b/solution.py
@@ -10,9 +10,14 @@
 
 TERMS = 6
 ROWS = 8
+SPLIT = 1
 LANES = 256
 F32 = jnp.float32
 BF16 = jnp.bfloat16
+
+
+def CUTS(each):
+    return [(0, each // 2), (each // 2, each)]
 
 
 def hop(value, mask):
@@ -35,27 +40,84 @@
         outs[k][...] = value[k * size : (k + 1) * size]
 
 
-def some_rows(fields, cholesky, far, block):
+def some_rows(fields, cholesky, far, block, cut, cuts):
     slots, vectors = fields.shape
-    columns = cholesky.shape[2]
+    columns = cholesky.shape[2] // cuts
     lanes = min(LANES, columns)
     size = slots // far
+    skip = cut * (columns // lanes)
     return pl.pallas_call(
         functools.partial(some_rows_kernel, far),
         grid=(columns // lanes,),
         in_specs=[
             pl.BlockSpec((slots, vectors), lambda t: (0, 0)),
-            pl.BlockSpec((vectors, ROWS, lanes), lambda t: (0, block, t)),
+            pl.BlockSpec((vectors, ROWS, lanes), lambda t: (0, block, skip + t)),
         ],
         out_specs=[pl.BlockSpec((size, ROWS, lanes), lambda t: (0, 0, t))] * far,
         out_shape=[jax.ShapeDtypeStruct((size, ROWS, columns), BF16)] * far,
-        compiler_params=pltpu.CompilerParams(vmem_limit_bytes=48 << 20),
+        compiler_params=pltpu.CompilerParams(vmem_limit_bytes=32 << 20),
         cost_estimate=pl.CostEstimate(
             flops=2 * slots * vectors * ROWS * columns,
             bytes_accessed=2 * vectors * ROWS * columns,
             transcendentals=0,
         ),
     )(fields, cholesky)
+
+
+def swap_kernel(chol, out):
+    out[...] = jnp.swapaxes(chol[...], 0, 1)
+
+
+def swapped_rows(cholesky, cut, cuts):
+    vectors, _, columns = cholesky.shape
+    columns //= cuts
+    lanes = min(LANES // 2, columns)
+    skip = cut * (columns // lanes)
+    return pl.pallas_call(
+        swap_kernel,
+        grid=(columns // lanes,),
+        in_specs=[pl.BlockSpec((vectors, ROWS, lanes), lambda t: (0, 0, skip + t))],
+        out_specs=pl.BlockSpec((ROWS, vectors, lanes), lambda t: (0, 0, t)),
+        out_shape=jax.ShapeDtypeStruct((ROWS, vectors, columns), BF16),
+        compiler_params=pltpu.CompilerParams(vmem_limit_bytes=24 << 20),
+        cost_estimate=pl.CostEstimate(
+            flops=0, bytes_accessed=2 * vectors * ROWS * columns, transcendentals=0
+        ),
+    )(cholesky)
+
+
+def swapped_kernel(far, parts, fields, *refs):
+    outs = refs[parts:]
+    size = fields.shape[0] // far
+    for p in range(parts):
+        columns = refs[p].shape[2]
+        value = [
+            jnp.dot(fields[...], refs[p][i], preferred_element_type=F32)
+            for i in range(ROWS)
+        ]
+        value = jnp.swapaxes(jnp.stack(value), 0, 1).astype(BF16)
+        for k in range(far):
+            outs[k][:, :, p * columns : (p + 1) * columns] = value[
+                k * size : (k + 1) * size
+            ]
+
+
+def first_rows(fields, blocks, far):
+    slots = fields.shape[0]
+    columns = sum(block.shape[2] for block in blocks)
+    space = pl.BlockSpec(memory_space=pltpu.VMEM)
+    return pl.pallas_call(
+        functools.partial(swapped_kernel, far, len(blocks)),
+        in_specs=[space] * (1 + len(blocks)),
+        out_specs=[space] * far,
+        out_shape=[jax.ShapeDtypeStruct((slots // far, ROWS, columns), BF16)] * far,
+        compiler_params=pltpu.CompilerParams(vmem_limit_bytes=32 << 20),
+        cost_estimate=pl.CostEstimate(
+            flops=2 * slots * blocks[0].shape[1] * ROWS * columns,
+            bytes_accessed=1 << 20,
+            transcendentals=0,
+        ),
+    )(fields, *blocks)
 
 
 def other_rows_kernel(near, far, cuts, fields, chol, *outs):
@@ -87,7 +149,7 @@
             jax.ShapeDtypeStruct(shape[:2] + (rows - done * ROWS, columns), BF16)
             for shape in shapes
         ],
-        compiler_params=pltpu.CompilerParams(vmem_limit_bytes=48 << 20),
+        compiler_params=pltpu.CompilerParams(vmem_limit_bytes=32 << 20),
         cost_estimate=pl.CostEstimate(
             flops=2 * slots * vectors * (rows - done * ROWS) * columns,
             bytes_accessed=2 * vectors * (rows - done * ROWS) * columns,
@@ -96,9 +158,13 @@
     )(fields, cholesky)
 
 
-def taylor_kernel(near, far, tops, has_rest, me_ref, *refs):
-    at = tops * near
-    first = [refs[i * near : (i + 1) * near] for i in range(tops)]
+def taylor_kernel(near, far, pieces, has_rest, walker, me_ref, *refs):
+    tops = len(pieces)
+    first = []
+    at = 0
+    for count in pieces:
+        first.append([refs[at + i * near : at + (i + 1) * near] for i in range(count)])
+        at += count * near
     rest = refs[at : at + far] if has_rest else None
     at += far if has_rest else 0
     start = refs[at : at + near]
@@ -107,7 +173,7 @@
     me = me_ref[0]
     group = len(terms)
     rows, electrons = terms[0].shape[1:]
-    columns = first[0][0].shape[-1]
+    columns = near * far * rows
     order = [(k, m) for k in range(far) for m in range(near)]
     spans = [(i * ROWS, (i + 1) * ROWS) for i in range(tops)]
     if has_rest:
@@ -117,19 +183,28 @@
         wide = [piece.astype(F32) for piece in pieces]
         return jnp.concatenate(wide, axis=0).astype(BF16)
 
+    opened = {
+        (k, m): jnp.swapaxes(start[m][k].astype(F32), 0, 1) for k, m in order
+    }
     matrices = []
     totals = []
     for w in range(group):
-        blocks = [joined([part[m][k, w] for k, m in order]) for part in first]
+        blocks = []
+        for part in first:
+            wide = [joined([cut[m][k, w] for k, m in order]) for cut in part]
+            blocks.append(jnp.concatenate(wide, axis=1))
         if has_rest:
             blocks.append(joined([rest[k][m, w] for k, m in order]))
         matrices.append(blocks)
         values = []
         for k, m in order:
-            side = (w % 2) * electrons
-            value = start[m][k, w // 2, :, side : side + electrons].astype(F32)
-            terms[w][me ^ (k * near + m)] = value
-            values.append(value)
+            pairs = opened[k, m][walker + w]
+            block = me ^ (k * near + m)
+            for side in range(2):
+                terms[w][block, pl.ds(side, rows // 2, stride=2), :] = pairs[
+                    :, side * electrons : (side + 1) * electrons
+                ]
+            values.append(terms[w][block])
         totals.append(
             [
                 jnp.concatenate([value[low:high] for value in values], axis=0)
@@ -150,32 +225,34 @@
                             i * size : (i + 1) * size
                         ]
     for i, (k, m) in enumerate(order):
-        pieces = []
+        whole = []
         for w in range(group):
             piece = [
                 totals[w][part][i * (high - low) : (i + 1) * (high - low)]
                 for part, (low, high) in enumerate(spans)
             ]
-            pieces.append(jnp.concatenate(piece, axis=0))
+            whole.append(jnp.concatenate(piece, axis=0))
         for w in range(0, group, 2):
-            outs[m][k, w // 2] = jnp.concatenate(pieces[w : w + 2], axis=1).astype(BF16)
+            outs[m][k, w // 2] = jnp.concatenate(whole[w : w + 2], axis=1).astype(BF16)
 
 
 def taylor(me, first, rest, start, low, high):
     near = len(start)
     far = start[0].shape[0]
-    columns = first[0][0].shape[3]
-    rows = start[0].shape[2]
+    rows = 2 * start[0].shape[1]
+    columns = near * far * rows
     electrons = start[0].shape[3] // 2
     pairs = (high - low) // 2
     group = high - low if high - low <= 4 and low % (high - low) == 0 else 2
     half = group // 2
+    args = [block for part in first for cut in part for block in cut]
     in_specs = [
         pl.BlockSpec(
-            (far, group, ROWS, columns), lambda i, me: (0, low // group + i, 0, 0)
+            (far, group, ROWS, block.shape[3]),
+            lambda i, me: (0, low // group + i, 0, 0),
         )
-    ] * (near * len(first))
-    args = [block for part in first for block in part]
+        for block in args
+    ]
     if rest is not None:
         in_specs += [
             pl.BlockSpec((near, group) + rest[0].shape[2:], lambda i, me: (0, i, 0, 0))
@@ -183,12 +260,19 @@
         args += list(rest)
     in_specs += [
         pl.BlockSpec(
-            (far, half, rows, 2 * electrons), lambda i, me: (0, low // group + i, 0, 0)
+            start[0].shape, lambda i, me: (0, 0, 0, 0)
         )
     ] * near
     args += list(start)
     return pl.pallas_call(
-        functools.partial(taylor_kernel, near, far, len(first), rest is not None),
+        functools.partial(
+            taylor_kernel,
+            near,
+            far,
+            [len(part) for part in first],
+            rest is not None,
+            low,
+        ),
         grid_spec=pltpu.PrefetchScalarGridSpec(
             num_scalar_prefetch=1,
             grid=((high - low) // group,),
@@ -200,7 +284,7 @@
             scratch_shapes=[pltpu.VMEM((near * far, rows, electrons), F32)] * group,
         ),
         out_shape=[jax.ShapeDtypeStruct((far, pairs, rows, 2 * electrons), BF16)] * near,
-        compiler_params=pltpu.CompilerParams(vmem_limit_bytes=40 << 20),
+        compiler_params=pltpu.CompilerParams(vmem_limit_bytes=32 << 20),
         cost_estimate=pl.CostEstimate(
             flops=20 * pairs * columns * columns * electrons,
             bytes_accessed=4 * pairs * columns * columns,
@@ -210,7 +294,10 @@
 
 
 def far_hops(blocks, near):
-    return [blocks[0]] + [hop(blocks[k], k * near) for k in range(1, len(blocks))]
+    got = list(blocks)
+    for k in sorted(range(1, len(blocks)), key=lambda k: -k.bit_length()):
+        got[k] = hop(blocks[k], k * near)
+    return got
 
 
 def near_hops(blocks):
@@ -248,10 +335,32 @@
         preferred_element_type=F32,
     ).astype(BF16)
 
-    def own(m):
-        return lax.dynamic_slice_in_dim(partial, (column ^ m) * chunk, chunk, 1)
-
-    bias = sum(part.astype(F32) for part in near_hops([own(m) for m in range(near)]))
+    def piece(c):
+        return lax.dynamic_slice_in_dim(partial, c * chunk, chunk, 1)
+
+    left = near // 2
+    side = column % 2
+    keep = [piece(2 * c + side) for c in range(left)]
+    give = [piece(2 * c + 1 - side) for c in range(left)]
+    shift = 1
+    while True:
+        got = hop(jnp.stack(give), shift)
+        total = [mine.astype(F32) + got[c].astype(F32) for c, mine in enumerate(keep)]
+        if left == 1:
+            break
+        shift *= 2
+        left //= 2
+        side = (column // shift) % 2
+        total = jnp.stack(total).astype(BF16)
+        keep = [
+            lax.dynamic_index_in_dim(total, 2 * c + side, 0, keepdims=False)
+            for c in range(left)
+        ]
+        give = [
+            lax.dynamic_index_in_dim(total, 2 * c + 1 - side, 0, keepdims=False)
+            for c in range(left)
+        ]
+    bias = total[0]
     shift = near
     while shift < devices:
         bias = bias.astype(BF16)
@@ -275,13 +384,20 @@
     select = jnp.dot(place, named, preferred_element_type=F32).astype(BF16)
     noise = jnp.dot(place, field_noise, preferred_element_type=F32)
 
-    start = jnp.dot(
-        select, walkers.reshape(count, rows * electrons), preferred_element_type=F32
+    start = jnp.einsum(
+        "sw,wpl->psl",
+        select,
+        walkers.reshape(count, rows // 2, 2 * electrons),
+        preferred_element_type=F32,
     ).astype(BF16)
-    start = start.reshape(far, near, each // 2, 2, rows, electrons)
-    start = start.transpose(0, 1, 2, 4, 3, 5)
-    start = start.reshape(far, near, each // 2, rows, 2 * electrons)
-    start = far_then_near([start[k] for k in range(far)], near, far)
+    start = start.reshape(rows // 2, far, near * each, 2 * electrons)
+    start = far_hops([start[:, k] for k in range(far)], near)
+    start = near_hops(
+        [
+            jnp.stack([part[:, m * each : (m + 1) * each] for part in start])
+            for m in range(near)
+        ],
+    )
 
     picked = jnp.dot(select, bias, preferred_element_type=F32)
     fields = noise + picked
@@ -289,17 +405,27 @@
     log_weight = jnp.sum(place.astype(F32) * weight[:, None], axis=0)
     fields = fields.astype(BF16)
 
-    shape = (near, each, ROWS, columns)
+    ahead = []
+    for cut in range(2):
+        ahead.append(swapped_rows(cholesky, cut, 2))
     tops = min(2, rows // ROWS)
     first = []
     for i in range(tops):
-        part = some_rows(fields, cholesky, far, i)
-        part = [block.reshape(shape) for block in part]
-        first.append(far_then_near(part, near, far))
+        parts = SPLIT if i == 0 and columns >= 2 * LANES else 1
+        first.append([])
+        for cut in range(parts):
+            if i == 0:
+                part = first_rows(fields, ahead, far)
+            else:
+                part = some_rows(fields, cholesky, far, i, cut, parts)
+            part = [
+                block.reshape(near, each, ROWS, columns // parts) for block in part
+            ]
+            first[i].append(far_then_near(part, near, far))
     blocks = None
     cuts = [(0, each)]
     if rows > tops * ROWS:
-        cuts = [(0, each // 2), (each // 2, each)]
+        cuts = CUTS(each)
         blocks = other_rows(fields, cholesky, near, far, cuts, tops)
     results = []
     for g, (low, high) in enumerate(cuts):

time: 218 us -> 217 us (level)
  waiting for transfers between devices: 115 us -> 101 us
  starting transfers between devices: 59.8 us -> 69 us
  Pallas kernels: 27.1 us -> 30.7 us
    ppermute x50 -> x49, waiting for transfers between devices: 115 us -> 101 us  [hop(): return lax.ppermute(value, 'orb', [(i, i ^ mask) for i in range(size)])]
    ppermute x50 -> x49, starting transfers between devices: 59.8 us -> 69 us  [hop(): return lax.ppermute(value, 'orb', [(i, i ^ mask) for i in range(size)])]
    pallas_call x2 -> x5, Pallas kernels: 6.16 us -> 14.5 us  [the longest x2 6.52 us: taylor(): pl.pallas_call(functools.partial(taylor_kernel, near, far, [len(part) for...]
    pallas_call x2 -> x1, Pallas kernels: 11.1 us -> 5.56 us  [some_rows(): pl.pallas_call(functools.partial(some_rows_kernel, far), grid=(columns //...]
    unnamed x8 -> x16, local copies, waits for them, and re-layouts: 1.01 us -> 5 us
  transfers between devices with their start and end apart: 50 -> 49, of which waited for: 20 -> 19; matrix products, arithmetic and copies ran while one was open for 4% -> 2% of each run, Pallas kernels for 12% -> 14%
where the time goes in v1:
time: 217 us
  waiting for transfers between devices  101 us (47%)
  starting transfers between devices  69 us (32%)
  Pallas kernels  30.7 us (14%)
  matrix products  6.16 us (3%)
  local copies, waits for them, and re-layouts  6.13 us (3%)
  other arithmetic  2.17 us (1%)
    ppermute x49, waiting for transfers between devices, hop(): return lax.ppermute(value, 'orb', [(i, i ^ mask) for i in range(size)])  101 us
    ppermute x49, starting transfers between devices, hop(): return lax.ppermute(value, 'orb', [(i, i ^ mask) for i in range(size)])  69 us
    pallas_call x1, Pallas kernels, other_rows(): pl.pallas_call(functools.partial(other_rows_kernel, near, far, cuts), gri...  10.6 us
    pallas_call x2, Pallas kernels, taylor(): pl.pallas_call(functools.partial(taylor_kernel, near, far, [len(part) for...  6.52 us
    pallas_call x2, Pallas kernels, swapped_rows(): pl.pallas_call(swap_kernel, grid=(columns // lanes,), in_specs=[pl.BlockS...  6.42 us
    pallas_call x1, Pallas kernels, some_rows(): pl.pallas_call(functools.partial(some_rows_kernel, far), grid=(columns //...  5.56 us
    unnamed x16, local copies, waits for them, and re-layouts  5 us
  transfers between devices with their start and end apart: 49, of which 19 were waited for; matrix products, arithmetic and copies ran while one was open for 2% of the time, Pallas kernels for 14%

profile of v1, /device:TPU:0, one launch (start us, length us, event | category | flops | bytes accessed | tf_op | source)
XLA Modules:
  0.0 216.8 jit_solution(1297028683899886973)
XLA Ops:
  1.7 2.9 %fusion = bf16[128,1024]{1,0:T(8,128)(2,1)S(1)} fusion(bf16[128,32,64]{0,2,1:T(8,128)(2,1)S(1)} %copy-done, bf16[1024,32,64]{0,2,1:T(8,128)(2,1)} %param.7), kind=kOutput, calls=%fused_computation.4 | convolution fusion | flops 537001984 | bytes 4980736 | tf_op jit(solution)/shard_map/dot_general | solution.py:331
  6.5 4.7 %collective-permute-start.27 = (bf16[16,32,128]{2,1,0:T(8,128)(2,1)S(1)}, bf16[16,32,128]{2,1,0:T(8,128)(2,1)S(1)}, u32[]{:S(2)}, u32[]{:S(2)}) collective-permute-start(bf16[16,32,128]{2,1,0:T(8,128)(2,1)S(1)} %get-tuple-element.57), channel_id=1, source_target_pairs={{0,12},{1,13},{2,14},{3,15},{4,8},{5,9},{6,10},{7,11},{8,4},{9,5},... | collective-permute-start | bytes 393224 | tf_op jit(solution)/shard_map/ppermute | solution.py:25
  11.9 3.2 %shard_map.68.refs_0_ = bf16[8,1024,256]{2,1,0:T(8,128)(2,1)S(1)} custom-call(bf16[1024,32,512]{2,1,0:T(8,128)(2,1)} %chol.7), custom_call_target="tpu_custom_call" | custom-call | bytes 4194304 | tf_op jit(solution)/shard_map/pallas_call | solution.py:76
  17.1 3.2 %shard_map.69.refs_1_ = bf16[8,1024,256]{2,1,0:T(8,128)(2,1)S(1)} custom-call(bf16[1024,32,512]{2,1,0:T(8,128)(2,1)} %chol.7), custom_call_target="tpu_custom_call" | custom-call | bytes 4194304 | tf_op jit(solution)/shard_map/pallas_call | solution.py:76
  24.4 2.4 %collective-permute-done.1 = bf16[1,128,256]{2,1,0:T(8,128)(2,1)S(1)} collective-permute-done((bf16[1,128,256]{2,1,0:T(8,128)(2,1)S(1)}, bf16[1,128,256]{2,1,0:T(8,128)(2,1)S(1)}, u32[]{:S(2)}, u32[]{:S(2)}) %collective-permute-start.1) | collective-permute-done | bytes 65568 | tf_op jit(solution)/shard_map/ppermute | solution.py:25
  31.2 2.3 %collective-permute-start.3 = (bf16[128,256]{1,0:T(8,128)(2,1)S(1)}, bf16[128,256]{1,0:T(8,128)(2,1)S(1)}, u32[]{:S(2)}, u32[]{:S(2)}) collective-permute-start(bf16[128,256]{1,0:T(8,128)(2,1)S(1)} %add_convert_fusion.1), channel_id=1, source_target_pairs={{0,8},{1,9},{2,10},{3,11},{4,12},{5,13},{6,14},{7,15},{8,0},{9,1},... | collective-permute-start | bytes 196616 | tf_op jit(solution)/shard_map/ppermute | solution.py:25
  33.5 2.9 %collective-permute-done.3 = bf16[128,256]{1,0:T(8,128)(2,1)S(1)} collective-permute-done((bf16[128,256]{1,0:T(8,128)(2,1)S(1)}, bf16[128,256]{1,0:T(8,128)(2,1)S(1)}, u32[]{:S(2)}, u32[]{:S(2)}) %collective-permute-start.3) | collective-permute-done | bytes 65568 | tf_op jit(solution)/shard_map/ppermute | solution.py:25
  38.4 2.3 %collective-permute-done.6 = bf16[128,256]{1,0:T(8,128)(2,1)S(1)} collective-permute-done((bf16[128,256]{1,0:T(8,128)(2,1)S(1)}, bf16[128,256]{1,0:T(8,128)(2,1)S(1)}, u32[]{:S(2)}, u32[]{:S(2)}) %collective-permute-start.6) | collective-permute-done | bytes 65568 | tf_op jit(solution)/shard_map/ppermute | solution.py:25
  43.0 5.6 %shard_map.71 = (bf16[32,8,512]{2,1,0:T(8,128)(2,1)S(1)}, bf16[32,8,512]{2,1,0:T(8,128)(2,1)S(1)}, bf16[32,8,512]{2,1,0:T(8,128)(2,1)S(1)}, bf16[32,8,512]{2,1,0:T(8,128)(2,1)S(1)}) custom-call(bf16[128,1024]{1,0:T(8,128)(2,1)S(1)} %get-tuple-element.53.fields, bf16[1024,32,512]{2,1,0:T(8,128)(2,1)} %chol.7), custom_call_target="tpu_custom_call" | custom-call | flops 1073741824 | bytes 8388608 | tf_op jit(solution)/shard_map/pallas_call | solution.py:49
  48.6 10.6 %shard_map.72 = (bf16[4,4,16,512]{3,2,1,0:T(8,128)(2,1)S(1)}, bf16[4,4,16,512]{3,2,1,0:T(8,128)(2,1)S(1)}, bf16[4,4,16,512]{3,2,1,0:T(8,128)(2,1)S(1)}, bf16[4,4...) custom-call(bf16[128,1024]{1,0:T(8,128)(2,1)S(1)} %get-tuple-element, ...), custom_call_target="tpu_custom_call" | custom-call | flops 2147483648 | bytes 16777216 | tf_op jit(solution)/shard_map/pallas_call | solution.py:138
  60.8 3.9 %collective-permute-start.9 = (bf16[4,8,8,512]{3,2,1,0:T(8,128)(2,1)S(1)}, bf16[4,8,8,512]{3,2,1,0:T(8,128)(2,1)S(1)}, u32[]{:S(2)}, u32[]{:S(2)}) collective-permute-start(bf16[4,8,8,512]{3,2,1,0:T(8,128)(2,1)S(1)} %bitcast.147), channel_id=1, source_target_pairs={{0,12},{1,13},{2,14},{3,15},{4,8},{5,9},{6,10},{7,11},{8,4},{9,5},... | collective-permute-start | bytes 786440 | tf_op jit(solution)/shard_map/ppermute | solution.py:25
  66.2 5.9 %collective-permute-done.9 = bf16[4,8,8,512]{3,2,1,0:T(8,128)(2,1)S(1)} collective-permute-done((bf16[4,8,8,512]{3,2,1,0:T(8,128)(2,1)S(1)}, bf16[4,8,8,512]{3,2,1,0:T(8,128)(2,1)S(1)}, u32[]{:S(2)}, u32[]{:S(2)}) %collective-permute-start.9) | collective-permute-done | bytes 262176 | tf_op jit(solution)/shard_map/ppermute | solution.py:25
  72.1 3.8 %collective-permute-start.15 = (bf16[4,8,8,512]{3,2,1,0:T(8,128)(2,1)S(1)}, bf16[4,8,8,512]{3,2,1,0:T(8,128)(2,1)S(1)}, u32[]{:S(2)}, u32[]{:S(2)}) collective-permute-start(bf16[4,8,8,512]{3,2,1,0:T(8,128)(2,1)S(1)} %bitcast.144), channel_id=1, source_target_pairs={{0,12},{1,13},{2,14},{3,15},{4,8},{5,9},{6,10},{7,11},{8,4},{9,5},... | collective-permute-start | bytes 786440 | tf_op jit(solution)/shard_map/ppermute | solution.py:25
  75.9 17.4 %collective-permute-done.8 = bf16[4,8,8,512]{3,2,1,0:T(8,128)(2,1)S(1)} collective-permute-done((bf16[4,8,8,512]{3,2,1,0:T(8,128)(2,1)S(1)}, bf16[4,8,8,512]{3,2,1,0:T(8,128)(2,1)S(1)}, u32[]{:S(2)}, u32[]{:S(2)}) %collective-permute-start.8) | collective-permute-done | bytes 262176 | tf_op jit(solution)/shard_map/ppermute | solution.py:25
  93.4 3.0 %collective-permute-start.13 = (bf16[4,8,8,512]{3,2,1,0:T(8,128)(2,1)S(1)}, bf16[4,8,8,512]{3,2,1,0:T(8,128)(2,1)S(1)}, u32[]{:S(2)}, u32[]{:S(2)}) collective-permute-start(bf16[4,8,8,512]{3,2,1,0:T(8,128)(2,1)S(1)} %bitcast.142), channel_id=1, source_target_pairs={{0,4},{1,5},{2,6},{3,7},{4,0},{5,1},{6,2},{7,3},{8,12},{9,13},{10,... | collective-permute-start | bytes 786440 | tf_op jit(solution)/shard_map/ppermute | solution.py:25
  96.5 12.7 %collective-permute-done.14 = bf16[4,8,8,512]{3,2,1,0:T(8,128)(2,1)S(1)} collective-permute-done((bf16[4,8,8,512]{3,2,1,0:T(8,128)(2,1)S(1)}, bf16[4,8,8,512]{3,2,1,0:T(8,128)(2,1)S(1)}, u32[]{:S(2)}, u32[]{:S(2)}) %collective-permute-start.14) | collective-permute-done | bytes 262176 | tf_op jit(solution)/shard_map/ppermute | solution.py:25
  111.6 6.8 %collective-permute-done.38 = bf16[4,4,16,512]{3,2,1,0:T(8,128)(2,1)S(1)} collective-permute-done((bf16[4,4,16,512]{3,2,1,0:T(8,128)(2,1)S(1)}, bf16[4,4,16,512]{3,2,1,0:T(8,128)(2,1)S(1)}, u32[]{:S(2)}, u32[]{:S(2)}) %collective-permute-start.38) | collective-permute-done | bytes 262176 | tf_op jit(solution)/shard_map/ppermute | solution.py:25
  119.6 2.9 %collective-permute-done.21 = bf16[4,4,16,512]{3,2,1,0:T(8,128)(2,1)S(1)} collective-permute-done((bf16[4,4,16,512]{3,2,1,0:T(8,128)(2,1)S(1)}, bf16[4,4,16,512]{3,2,1,0:T(8,128)(2,1)S(1)}, u32[]{:S(2)}, u32[]{:S(2)}) %collective-permute-start.21) | collective-permute-done | bytes 262176 | tf_op jit(solution)/shard_map/ppermute | solution.py:25
  124.0 3.8 %collective-permute-done.20 = bf16[4,4,16,512]{3,2,1,0:T(8,128)(2,1)S(1)} collective-permute-done((bf16[4,4,16,512]{3,2,1,0:T(8,128)(2,1)S(1)}, bf16[4,4,16,512]{3,2,1,0:T(8,128)(2,1)S(1)}, u32[]{:S(2)}, u32[]{:S(2)}) %collective-permute-start.20) | collective-permute-done | bytes 262176 | tf_op jit(solution)/shard_map/ppermute | solution.py:25
  131.1 10.3 %collective-permute-done.30.refs_15_ = bf16[4,16,8,128]{3,2,1,0:T(8,128)(2,1)S(1)} collective-permute-done((bf16[4,16,8,128]{3,2,1,0:T(8,128)(2,1)S(1)}, bf16[4,16,8,128]{3,2,1,0:T(8,128)(2,1)S(1)}, u32[]{:S(2)}, u32[]{:S(2)}) %collective-permute-start.30) | collective-permute-done | bytes 131104 | tf_op jit(solution)/shard_map/ppermute | solution.py:25
  143.9 3.6 %collective-permute-start.40 = (bf16[4,4,16,512]{3,2,1,0:T(8,128)(2,1)S(1)}, bf16[4,4,16,512]{3,2,1,0:T(8,128)(2,1)S(1)}, u32[]{:S(2)}, u32[]{:S(2)}) collective-permute-start(bf16[4,4,16,512]{3,2,1,0:T(8,128)(2,1)S(1)} %pad_maximum_fusion.14), channel_id=1, source_target_pairs={{0,4},{1,5},{2,6},{3,7},{4,0},{5,1},{6,2},{7,3},{8,12},{9,13},{10,... | collective-permute-start | bytes 786440 | tf_op jit(solution)/shard_map/ppermute | solution.py:25
  150.3 4.8 %collective-permute-start.22 = (bf16[4,4,16,512]{3,2,1,0:T(8,128)(2,1)S(1)}, bf16[4,4,16,512]{3,2,1,0:T(8,128)(2,1)S(1)}, u32[]{:S(2)}, u32[]{:S(2)}) collective-permute-start(bf16[4,4,16,512]{3,2,1,0:T(8,128)(2,1)S(1)} %pad_maximum_fusion.10), channel_id=1, source_target_pairs={{0,4},{1,5},{2,6},{3,7},{4,0},{5,1},{6,2},{7,3},{8,12},{9,13},{10,... | collective-permute-start | bytes 786440 | tf_op jit(solution)/shard_map/ppermute | solution.py:25
  156.2 4.1 %collective-permute-start.23 = (bf16[4,4,16,512]{3,2,1,0:T(8,128)(2,1)S(1)}, bf16[4,4,16,512]{3,2,1,0:T(8,128)(2,1)S(1)}, u32[]{:S(2)}, u32[]{:S(2)}) collective-permute-start(bf16[4,4,16,512]{3,2,1,0:T(8,128)(2,1)S(1)} %pad_maximum_fusion.11), channel_id=1, source_target_pairs={{0,8},{1,9},{2,10},{3,11},{4,12},{5,13},{6,14},{7,15},{8,0},{9,1},... | collective-permute-start | bytes 786440 | tf_op jit(solution)/shard_map/ppermute | solution.py:25
  161.8 7.2 %collective-permute-done.41.refs_10_ = bf16[4,4,16,512]{3,2,1,0:T(8,128)(2,1)S(1)} collective-permute-done((bf16[4,4,16,512]{3,2,1,0:T(8,128)(2,1)S(1)}, bf16[4,4,16,512]{3,2,1,0:T(8,128)(2,1)S(1)}, u32[]{:S(2)}, u32[]{:S(2)}) %collective-permute-start.41) | collective-permute-done | bytes 262176 | tf_op jit(solution)/shard_map/ppermute | solution.py:25
  169.0 3.3 %shard_map.74 = (bf16[4,2,32,128]{3,2,1,0:T(8,128)(2,1)S(1)}, bf16[4,2,32,128]{3,2,1,0:T(8,128)(2,1)S(1)}, bf16[4,2,32,128]{3,2,1,0:T(8,128)(2,1)S(1)}, bf16[4,2,32,128]{3,2,1,0:T(8,128)(2,1)S(1)}) custom-call(s32[1]{0:T(128)} %bitcast.3.me_ref, bf16[4,8,8,512]{3,2,1,0:T(8,128)(2,1)S(1)} %get-tuple-element.183.refs_0_, ...), custom_call_target="tpu_custom_call" | custom-call | flops 671088640 | bytes 2097152 | tf_op jit(solution)/shard_map/pallas_call | solution.py:267
  174.3 17.2 %collective-permute-done.23.refs_10_ = bf16[4,4,16,512]{3,2,1,0:T(8,128)(2,1)S(1)} collective-permute-done((bf16[4,4,16,512]{3,2,1,0:T(8,128)(2,1)S(1)}, bf16[4,4,16,512]{3,2,1,0:T(8,128)(2,1)S(1)}, u32[]{:S(2)}, u32[]{:S(2)}) %collective-permute-start.23) | collective-permute-done | bytes 262176 | tf_op jit(solution)/shard_map/ppermute | solution.py:25
  191.5 3.3 %shard_map.73 = (bf16[4,2,32,128]{3,2,1,0:T(8,128)(2,1)S(1)}, bf16[4,2,32,128]{3,2,1,0:T(8,128)(2,1)S(1)}, bf16[4,2,32,128]{3,2,1,0:T(8,128)(2,1)S(1)}, bf16[4,2,32,128]{3,2,1,0:T(8,128)(2,1)S(1)}) custom-call(s32[1]{0:T(128)} %bitcast.3.me_ref, bf16[4,8,8,512]{3,2,1,0:T(8,128)(2,1)S(1)} %get-tuple-element.183.refs_0_, ...), custom_call_target="tpu_custom_call" | custom-call | flops 671088640 | bytes 2097152 | tf_op jit(solution)/shard_map/pallas_call | solution.py:267
  196.8 2.4 %collective-permute-start.48 = (bf16[4,2,32,128]{3,2,1,0:T(8,128)(2,1)S(1)}, bf16[4,2,32,128]{3,2,1,0:T(8,128)(2,1)S(1)}, u32[]{:S(2)}, u32[]{:S(2)}) collective-permute-start(bf16[4,2,32,128]{3,2,1,0:T(8,128)(2,1)S(1)} %pad_maximum_fusion.27), channel_id=1, source_target_pairs={{0,12},{1,13},{2,14},{3,15},{4,8},{5,9},{6,10},{7,11},{8,4},{9,5},... | collective-permute-start | bytes 196616 | tf_op jit(solution)/shard_map/ppermute | solution.py:25
  199.2 4.6 %collective-permute-start.47 = (bf16[4,2,32,128]{3,2,1,0:T(8,128)(2,1)S(1)}, bf16[4,2,32,128]{3,2,1,0:T(8,128)(2,1)S(1)}, u32[]{:S(2)}, u32[]{:S(2)}) collective-permute-start(bf16[4,2,32,128]{3,2,1,0:T(8,128)(2,1)S(1)} %pad_maximum_fusion.26), channel_id=1, source_target_pairs={{0,8},{1,9},{2,10},{3,11},{4,12},{5,13},{6,14},{7,15},{8,0},{9,1},... | collective-permute-start | bytes 196616 | tf_op jit(solution)/shard_map/ppermute | solution.py:25
  204.4 2.5 %collective-permute-start.36 = (bf16[4,2,32,128]{3,2,1,0:T(8,128)(2,1)S(1)}, bf16[4,2,32,128]{3,2,1,0:T(8,128)(2,1)S(1)}, u32[]{:S(2)}, u32[]{:S(2)}) collective-permute-start(bf16[4,2,32,128]{3,2,1,0:T(8,128)(2,1)S(1)} %pad_maximum_fusion.24), channel_id=1, source_target_pairs={{0,12},{1,13},{2,14},{3,15},{4,8},{5,9},{6,10},{7,11},{8,4},{9,5},... | collective-permute-start | bytes 196616 | tf_op jit(solution)/shard_map/ppermute | solution.py:25
  209.6 2.2 %collective-permute-done.36 = bf16[4,2,32,128]{3,2,1,0:T(8,128)(2,1)S(1)} collective-permute-done((bf16[4,2,32,128]{3,2,1,0:T(8,128)(2,1)S(1)}, bf16[4,2,32,128]{3,2,1,0:T(8,128)(2,1)S(1)}, u32[]{:S(2)}, u32[]{:S(2)}) %collective-permute-start.36) | collective-permute-done | bytes 65568 | tf_op jit(solution)/shard_map/ppermute | solution.py:25
  211.8 2.3 %collective-permute-done.35 = bf16[4,2,32,128]{3,2,1,0:T(8,128)(2,1)S(1)} collective-permute-done((bf16[4,2,32,128]{3,2,1,0:T(8,128)(2,1)S(1)}, bf16[4,2,32,128]{3,2,1,0:T(8,128)(2,1)S(1)}, u32[]{:S(2)}, u32[]{:S(2)}) %collective-permute-start.35) | collective-permute-done | bytes 65568 | tf_op jit(solution)/shard_map/ppermute | solution.py:25
  (170 shorter events, 47.1 us)
Async XLA Ops:
  4.7 17.7 %collective-permute-start = (bf16[2,128,256]{2,1,0:T(8,128)(2,1)S(1)}, bf16[2,128,256]{2,1,0:T(8,128)(2,1)S(1)}, u32[]{:S(2)}, u32[]{:S(2)}) collective-permute-start(bf16[2,128,256]{2,1,0:T(8,128)(2,1)S(1)} %pad_maximum_fusion.17), channel_id=1, source_target_pairs={{0,1},{1,0},{2,3},{3,2},{4,5},{5,4},{6,7},{7,6},{8,9},{9,8},{10,11... | collective-permute-start | bytes 393224 | tf_op jit(solution)/shard_map/ppermute | solution.py:25
  6.5 17.7 %collective-permute-start.27 = (bf16[16,32,128]{2,1,0:T(8,128)(2,1)S(1)}, bf16[16,32,128]{2,1,0:T(8,128)(2,1)S(1)}, u32[]{:S(2)}, u32[]{:S(2)}) collective-permute-start(bf16[16,32,128]{2,1,0:T(8,128)(2,1)S(1)} %get-tuple-element.57), channel_id=1, source_target_pairs={{0,12},{1,13},{2,14},{3,15},{4,8},{5,9},{6,10},{7,11},{8,4},{9,5},... | collective-permute-start | bytes 393224 | tf_op jit(solution)/shard_map/ppermute | solution.py:25
  11.2 13.1 %collective-permute-start.26 = (bf16[16,32,128]{2,1,0:T(8,128)(2,1)S(1)}, bf16[16,32,128]{2,1,0:T(8,128)(2,1)S(1)}, u32[]{:S(2)}, u32[]{:S(2)}) collective-permute-start(bf16[16,32,128]{2,1,0:T(8,128)(2,1)S(1)} %get-tuple-element.55), channel_id=1, source_target_pairs={{0,8},{1,9},{2,10},{3,11},{4,12},{5,13},{6,14},{7,15},{8,0},{9,1},... | collective-permute-start | bytes 393224 | tf_op jit(solution)/shard_map/ppermute | solution.py:25
  11.2 13.1 %collective-permute-start.25 = (bf16[16,32,128]{2,1,0:T(8,128)(2,1)S(1)}, bf16[16,32,128]{2,1,0:T(8,128)(2,1)S(1)}, u32[]{:S(2)}, u32[]{:S(2)}) collective-permute-start(bf16[16,32,128]{2,1,0:T(8,128)(2,1)S(1)} %get-tuple-element.56), channel_id=1, source_target_pairs={{0,4},{1,5},{2,6},{3,7},{4,0},{5,1},{6,2},{7,3},{8,12},{9,13},{10,... | collective-permute-start | bytes 393224 | tf_op jit(solution)/shard_map/ppermute | solution.py:25
  24.3 104.7 %collective-permute-start.28 = (bf16[4,16,8,128]{3,2,1,0:T(8,128)(2,1)S(1)}, bf16[4,16,8,128]{3,2,1,0:T(8,128)(2,1)S(1)}, u32[]{:S(2)}, u32[]{:S(2)}) collective-permute-start(bf16[4,16,8,128]{3,2,1,0:T(8,128)(2,1)S(1)} %pad_maximum_fusion.19), channel_id=1, source_target_pairs={{0,1},{1,0},{2,3},{3,2},{4,5},{5,4},{6,7},{7,6},{8,9},{9,8},{10,11... | collective-permute-start | bytes 393224 | tf_op jit(solution)/shard_map/ppermute | solution.py:25
  28.3 102.0 %collective-permute-start.29 = (bf16[4,16,8,128]{3,2,1,0:T(8,128)(2,1)S(1)}, bf16[4,16,8,128]{3,2,1,0:T(8,128)(2,1)S(1)}, u32[]{:S(2)}, u32[]{:S(2)}) collective-permute-start(bf16[4,16,8,128]{3,2,1,0:T(8,128)(2,1)S(1)} %pad_maximum_fusion.20), channel_id=1, source_target_pairs={{0,2},{1,3},{2,0},{3,1},{4,6},{5,7},{6,4},{7,5},{8,10},{9,11},{10,... | collective-permute-start | bytes 393224 | tf_op jit(solution)/shard_map/ppermute | solution.py:25
  60.8 11.2 %collective-permute-start.9 = (bf16[4,8,8,512]{3,2,1,0:T(8,128)(2,1)S(1)}, bf16[4,8,8,512]{3,2,1,0:T(8,128)(2,1)S(1)}, u32[]{:S(2)}, u32[]{:S(2)}) collective-permute-start(bf16[4,8,8,512]{3,2,1,0:T(8,128)(2,1)S(1)} %bitcast.147), channel_id=1, source_target_pairs={{0,12},{1,13},{2,14},{3,15},{4,8},{5,9},{6,10},{7,11},{8,4},{9,5},... | collective-permute-start | bytes 786440 | tf_op jit(solution)/shard_map/ppermute | solution.py:25
  64.8 28.6 %collective-permute-start.8 = (bf16[4,8,8,512]{3,2,1,0:T(8,128)(2,1)S(1)}, bf16[4,8,8,512]{3,2,1,0:T(8,128)(2,1)S(1)}, u32[]{:S(2)}, u32[]{:S(2)}) collective-permute-start(bf16[4,8,8,512]{3,2,1,0:T(8,128)(2,1)S(1)} %bitcast.146), channel_id=1, source_target_pairs={{0,8},{1,9},{2,10},{3,11},{4,12},{5,13},{6,14},{7,15},{8,0},{9,1},... | collective-permute-start | bytes 786440 | tf_op jit(solution)/shard_map/ppermute | solution.py:25
  64.8 28.6 %collective-permute-start.7 = (bf16[4,8,8,512]{3,2,1,0:T(8,128)(2,1)S(1)}, bf16[4,8,8,512]{3,2,1,0:T(8,128)(2,1)S(1)}, u32[]{:S(2)}, u32[]{:S(2)}) collective-permute-start(bf16[4,8,8,512]{3,2,1,0:T(8,128)(2,1)S(1)} %bitcast.145), channel_id=1, source_target_pairs={{0,4},{1,5},{2,6},{3,7},{4,0},{5,1},{6,2},{7,3},{8,12},{9,13},{10,... | collective-permute-start | bytes 786440 | tf_op jit(solution)/shard_map/ppermute | solution.py:25
  72.1 24.3 %collective-permute-start.15 = (bf16[4,8,8,512]{3,2,1,0:T(8,128)(2,1)S(1)}, bf16[4,8,8,512]{3,2,1,0:T(8,128)(2,1)S(1)}, u32[]{:S(2)}, u32[]{:S(2)}) collective-permute-start(bf16[4,8,8,512]{3,2,1,0:T(8,128)(2,1)S(1)} %bitcast.144), channel_id=1, source_target_pairs={{0,12},{1,13},{2,14},{3,15},{4,8},{5,9},{6,10},{7,11},{8,4},{9,5},... | collective-permute-start | bytes 786440 | tf_op jit(solution)/shard_map/ppermute | solution.py:25
  93.3 15.9 %collective-permute-start.14 = (bf16[4,8,8,512]{3,2,1,0:T(8,128)(2,1)S(1)}, bf16[4,8,8,512]{3,2,1,0:T(8,128)(2,1)S(1)}, u32[]{:S(2)}, u32[]{:S(2)}) collective-permute-start(bf16[4,8,8,512]{3,2,1,0:T(8,128)(2,1)S(1)} %bitcast.143), channel_id=1, source_target_pairs={{0,8},{1,9},{2,10},{3,11},{4,12},{5,13},{6,14},{7,15},{8,0},{9,1},... | collective-permute-start | bytes 786440 | tf_op jit(solution)/shard_map/ppermute | solution.py:25
  93.4 16.8 %collective-permute-start.13 = (bf16[4,8,8,512]{3,2,1,0:T(8,128)(2,1)S(1)}, bf16[4,8,8,512]{3,2,1,0:T(8,128)(2,1)S(1)}, u32[]{:S(2)}, u32[]{:S(2)}) collective-permute-start(bf16[4,8,8,512]{3,2,1,0:T(8,128)(2,1)S(1)} %bitcast.142), channel_id=1, source_target_pairs={{0,4},{1,5},{2,6},{3,7},{4,0},{5,1},{6,2},{7,3},{8,12},{9,13},{10,... | collective-permute-start | bytes 786440 | tf_op jit(solution)/shard_map/ppermute | solution.py:25
  96.4 13.9 %collective-permute-start.39 = (bf16[4,4,16,512]{3,2,1,0:T(8,128)(2,1)S(1)}, bf16[4,4,16,512]{3,2,1,0:T(8,128)(2,1)S(1)}, u32[]{:S(2)}, u32[]{:S(2)}) collective-permute-start(bf16[4,4,16,512]{3,2,1,0:T(8,128)(2,1)S(1)} %get-tuple-element.45), channel_id=1, source_target_pairs={{0,3},{1,2},{2,1},{3,0},{4,7},{5,6},{6,5},{7,4},{8,11},{9,10},{10,... | collective-permute-start | bytes 786440 | tf_op jit(solution)/shard_map/ppermute | solution.py:25
  110.3 12.1 %collective-permute-start.21 = (bf16[4,4,16,512]{3,2,1,0:T(8,128)(2,1)S(1)}, bf16[4,4,16,512]{3,2,1,0:T(8,128)(2,1)S(1)}, u32[]{:S(2)}, u32[]{:S(2)}) collective-permute-start(bf16[4,4,16,512]{3,2,1,0:T(8,128)(2,1)S(1)} %get-tuple-element.37), channel_id=1, source_target_pairs={{0,3},{1,2},{2,1},{3,0},{4,7},{5,6},{6,5},{7,4},{8,11},{9,10},{10,... | collective-permute-start | bytes 786440 | tf_op jit(solution)/shard_map/ppermute | solution.py:25
  122.4 19.9 %collective-permute-start.10 = (bf16[4,8,8,512]{3,2,1,0:T(8,128)(2,1)S(1)}, bf16[4,8,8,512]{3,2,1,0:T(8,128)(2,1)S(1)}, u32[]{:S(2)}, u32[]{:S(2)}) collective-permute-start(bf16[4,8,8,512]{3,2,1,0:T(8,128)(2,1)S(1)} %pad_maximum_fusion.2), channel_id=1, source_target_pairs={{0,1},{1,0},{2,3},{3,2},{4,5},{5,4},{6,7},{7,6},{8,9},{9,8},{10,11... | collective-permute-start | bytes 786440 | tf_op jit(solution)/shard_map/ppermute | solution.py:25
  127.8 16.1 %collective-permute-start.11 = (bf16[4,8,8,512]{3,2,1,0:T(8,128)(2,1)S(1)}, bf16[4,8,8,512]{3,2,1,0:T(8,128)(2,1)S(1)}, u32[]{:S(2)}, u32[]{:S(2)}) collective-permute-start(bf16[4,8,8,512]{3,2,1,0:T(8,128)(2,1)S(1)} %pad_maximum_fusion.3), channel_id=1, source_target_pairs={{0,2},{1,3},{2,0},{3,1},{4,6},{5,7},{6,4},{7,5},{8,10},{9,11},{10,... | collective-permute-start | bytes 786440 | tf_op jit(solution)/shard_map/ppermute | solution.py:25
  128.9 18.7 %collective-permute-start.12 = (bf16[4,8,8,512]{3,2,1,0:T(8,128)(2,1)S(1)}, bf16[4,8,8,512]{3,2,1,0:T(8,128)(2,1)S(1)}, u32[]{:S(2)}, u32[]{:S(2)}) collective-permute-start(bf16[4,8,8,512]{3,2,1,0:T(8,128)(2,1)S(1)} %pad_maximum_fusion.4), channel_id=1, source_target_pairs={{0,3},{1,2},{2,1},{3,0},{4,7},{5,6},{6,5},{7,4},{8,11},{9,10},{10,... | collective-permute-start | bytes 786440 | tf_op jit(solution)/shard_map/ppermute | solution.py:25
  129.1 19.5 %collective-permute-start.16 = (bf16[4,8,8,512]{3,2,1,0:T(8,128)(2,1)S(1)}, bf16[4,8,8,512]{3,2,1,0:T(8,128)(2,1)S(1)}, u32[]{:S(2)}, u32[]{:S(2)}) collective-permute-start(bf16[4,8,8,512]{3,2,1,0:T(8,128)(2,1)S(1)} %pad_maximum_fusion.6), channel_id=1, source_target_pairs={{0,1},{1,0},{2,3},{3,2},{4,5},{5,4},{6,7},{7,6},{8,9},{9,8},{10,11... | collective-permute-start | bytes 786440 | tf_op jit(solution)/shard_map/ppermute | solution.py:25
  130.3 11.1 %collective-permute-start.30 = (bf16[4,16,8,128]{3,2,1,0:T(8,128)(2,1)S(1)}, bf16[4,16,8,128]{3,2,1,0:T(8,128)(2,1)S(1)}, u32[]{:S(2)}, u32[]{:S(2)}) collective-permute-start(bf16[4,16,8,128]{3,2,1,0:T(8,128)(2,1)S(1)} %pad_maximum_fusion.21), channel_id=1, source_target_pairs={{0,3},{1,2},{2,1},{3,0},{4,7},{5,6},{6,5},{7,4},{8,11},{9,10},{10,... | collective-permute-start | bytes 393224 | tf_op jit(solution)/shard_map/ppermute | solution.py:25
  142.3 13.9 %collective-permute-start.18 = (bf16[4,8,8,512]{3,2,1,0:T(8,128)(2,1)S(1)}, bf16[4,8,8,512]{3,2,1,0:T(8,128)(2,1)S(1)}, u32[]{:S(2)}, u32[]{:S(2)}) collective-permute-start(bf16[4,8,8,512]{3,2,1,0:T(8,128)(2,1)S(1)} %pad_maximum_fusion.8), channel_id=1, source_target_pairs={{0,3},{1,2},{2,1},{3,0},{4,7},{5,6},{6,5},{7,4},{8,11},{9,10},{10,... | collective-permute-start | bytes 786440 | tf_op jit(solution)/shard_map/ppermute | solution.py:25
  143.9 16.3 %collective-permute-start.40 = (bf16[4,4,16,512]{3,2,1,0:T(8,128)(2,1)S(1)}, bf16[4,4,16,512]{3,2,1,0:T(8,128)(2,1)S(1)}, u32[]{:S(2)}, u32[]{:S(2)}) collective-permute-start(bf16[4,4,16,512]{3,2,1,0:T(8,128)(2,1)S(1)} %pad_maximum_fusion.14), channel_id=1, source_target_pairs={{0,4},{1,5},{2,6},{3,7},{4,0},{5,1},{6,2},{7,3},{8,12},{9,13},{10,... | collective-permute-start | bytes 786440 | tf_op jit(solution)/shard_map/ppermute | solution.py:25
  147.6 21.4 %collective-permute-start.41 = (bf16[4,4,16,512]{3,2,1,0:T(8,128)(2,1)S(1)}, bf16[4,4,16,512]{3,2,1,0:T(8,128)(2,1)S(1)}, u32[]{:S(2)}, u32[]{:S(2)}) collective-permute-start(bf16[4,4,16,512]{3,2,1,0:T(8,128)(2,1)S(1)} %pad_maximum_fusion.15), channel_id=1, source_target_pairs={{0,8},{1,9},{2,10},{3,11},{4,12},{5,13},{6,14},{7,15},{8,0},{9,1},... | collective-permute-start | bytes 786440 | tf_op jit(solution)/shard_map/ppermute | solution.py:25
  148.5 20.5 %collective-permute-start.42 = (bf16[4,4,16,512]{3,2,1,0:T(8,128)(2,1)S(1)}, bf16[4,4,16,512]{3,2,1,0:T(8,128)(2,1)S(1)}, u32[]{:S(2)}, u32[]{:S(2)}) collective-permute-start(bf16[4,4,16,512]{3,2,1,0:T(8,128)(2,1)S(1)} %pad_maximum_fusion.16), channel_id=1, source_target_pairs={{0,12},{1,13},{2,14},{3,15},{4,8},{5,9},{6,10},{7,11},{8,4},{9,5},... | collective-permute-start | bytes 786440 | tf_op jit(solution)/shard_map/ppermute | solution.py:25
  150.3 23.3 %collective-permute-start.22 = (bf16[4,4,16,512]{3,2,1,0:T(8,128)(2,1)S(1)}, bf16[4,4,16,512]{3,2,1,0:T(8,128)(2,1)S(1)}, u32[]{:S(2)}, u32[]{:S(2)}) collective-permute-start(bf16[4,4,16,512]{3,2,1,0:T(8,128)(2,1)S(1)} %pad_maximum_fusion.10), channel_id=1, source_target_pairs={{0,4},{1,5},{2,6},{3,7},{4,0},{5,1},{6,2},{7,3},{8,12},{9,13},{10,... | collective-permute-start | bytes 786440 | tf_op jit(solution)/shard_map/ppermute | solution.py:25
  156.2 35.3 %collective-permute-start.23 = (bf16[4,4,16,512]{3,2,1,0:T(8,128)(2,1)S(1)}, bf16[4,4,16,512]{3,2,1,0:T(8,128)(2,1)S(1)}, u32[]{:S(2)}, u32[]{:S(2)}) collective-permute-start(bf16[4,4,16,512]{3,2,1,0:T(8,128)(2,1)S(1)} %pad_maximum_fusion.11), channel_id=1, source_target_pairs={{0,8},{1,9},{2,10},{3,11},{4,12},{5,13},{6,14},{7,15},{8,0},{9,1},... | collective-permute-start | bytes 786440 | tf_op jit(solution)/shard_map/ppermute | solution.py:25
  160.3 31.2 %collective-permute-start.24 = (bf16[4,4,16,512]{3,2,1,0:T(8,128)(2,1)S(1)}, bf16[4,4,16,512]{3,2,1,0:T(8,128)(2,1)S(1)}, u32[]{:S(2)}, u32[]{:S(2)}) collective-permute-start(bf16[4,4,16,512]{3,2,1,0:T(8,128)(2,1)S(1)} %pad_maximum_fusion.12), channel_id=1, source_target_pairs={{0,12},{1,13},{2,14},{3,15},{4,8},{5,9},{6,10},{7,11},{8,4},{9,5},... | collective-permute-start | bytes 786440 | tf_op jit(solution)/shard_map/ppermute | solution.py:25
  172.3 23.8 %collective-permute-start.45 = (bf16[4,2,32,128]{3,2,1,0:T(8,128)(2,1)S(1)}, bf16[4,2,32,128]{3,2,1,0:T(8,128)(2,1)S(1)}, u32[]{:S(2)}, u32[]{:S(2)}) collective-permute-start(bf16[4,2,32,128]{3,2,1,0:T(8,128)(2,1)S(1)} %get-tuple-element.49), channel_id=1, source_target_pairs={{0,3},{1,2},{2,1},{3,0},{4,7},{5,6},{6,5},{7,4},{8,11},{9,10},{10,... | collective-permute-start | bytes 196616 | tf_op jit(solution)/shard_map/ppermute | solution.py:25
  172.3 24.4 %collective-permute-start.44 = (bf16[4,2,32,128]{3,2,1,0:T(8,128)(2,1)S(1)}, bf16[4,2,32,128]{3,2,1,0:T(8,128)(2,1)S(1)}, u32[]{:S(2)}, u32[]{:S(2)}) collective-permute-start(bf16[4,2,32,128]{3,2,1,0:T(8,128)(2,1)S(1)} %get-tuple-element.48), channel_id=1, source_target_pairs={{0,2},{1,3},{2,0},{3,1},{4,6},{5,7},{6,4},{7,5},{8,10},{9,11},{10,... | collective-permute-start | bytes 196616 | tf_op jit(solution)/shard_map/ppermute | solution.py:25
  173.6 23.1 %collective-permute-start.43 = (bf16[4,2,32,128]{3,2,1,0:T(8,128)(2,1)S(1)}, bf16[4,2,32,128]{3,2,1,0:T(8,128)(2,1)S(1)}, u32[]{:S(2)}, u32[]{:S(2)}) collective-permute-start(bf16[4,2,32,128]{3,2,1,0:T(8,128)(2,1)S(1)} %get-tuple-element.47), channel_id=1, source_target_pairs={{0,1},{1,0},{2,3},{3,2},{4,5},{5,4},{6,7},{7,6},{8,9},{9,8},{10,11... | collective-permute-start | bytes 196616 | tf_op jit(solution)/shard_map/ppermute | solution.py:25
  194.8 9.5 %collective-permute-start.32 = (bf16[4,2,32,128]{3,2,1,0:T(8,128)(2,1)S(1)}, bf16[4,2,32,128]{3,2,1,0:T(8,128)(2,1)S(1)}, u32[]{:S(2)}, u32[]{:S(2)}) collective-permute-start(bf16[4,2,32,128]{3,2,1,0:T(8,128)(2,1)S(1)} %get-tuple-element.40), channel_id=1, source_target_pairs={{0,2},{1,3},{2,0},{3,1},{4,6},{5,7},{6,4},{7,5},{8,10},{9,11},{10,... | collective-permute-start | bytes 196616 | tf_op jit(solution)/shard_map/ppermute | solution.py:25
  196.8 10.8 %collective-permute-start.48 = (bf16[4,2,32,128]{3,2,1,0:T(8,128)(2,1)S(1)}, bf16[4,2,32,128]{3,2,1,0:T(8,128)(2,1)S(1)}, u32[]{:S(2)}, u32[]{:S(2)}) collective-permute-start(bf16[4,2,32,128]{3,2,1,0:T(8,128)(2,1)S(1)} %pad_maximum_fusion.27), channel_id=1, source_target_pairs={{0,12},{1,13},{2,14},{3,15},{4,8},{5,9},{6,10},{7,11},{8,4},{9,5},... | collective-permute-start | bytes 196616 | tf_op jit(solution)/shard_map/ppermute | solution.py:25
  199.2 10.4 %collective-permute-start.47 = (bf16[4,2,32,128]{3,2,1,0:T(8,128)(2,1)S(1)}, bf16[4,2,32,128]{3,2,1,0:T(8,128)(2,1)S(1)}, u32[]{:S(2)}, u32[]{:S(2)}) collective-permute-start(bf16[4,2,32,128]{3,2,1,0:T(8,128)(2,1)S(1)} %pad_maximum_fusion.26), channel_id=1, source_target_pairs={{0,8},{1,9},{2,10},{3,11},{4,12},{5,13},{6,14},{7,15},{8,0},{9,1},... | collective-permute-start | bytes 196616 | tf_op jit(solution)/shard_map/ppermute | solution.py:25
  (25 other events, 194.9 us)
